TPU v7x, 256 devices: a whole 4x4x8 slice. The times are simulated.
256 devices in a mesh: dom: 32 (over z, x), rep: 8 (over y, core).
Axes of the slice: x: 4, y: 4, z: 8, core: 2. Of those that a mesh axis runs over, the one named last changes fastest.
Arguments:
- grad_out: bfloat16 [262144, 512], P(('dom', 'rep')), may hold values from -6 to 6
- features: bfloat16 [262144, 512], P(('dom', 'rep')), may hold values from -24 to 24
- weight: bfloat16 [512, 512], replicated, may hold values from -0.25 to 0.25
- edge_blocks: bfloat16 [32768, 128, 128], P(('dom', 'rep')), may hold values from -0.25 to 0.25
- block_index: int32 [32768, 2], P(('dom', 'rep')), may hold values from 0 to 63, as said below
- block_count: int32 [256], P(('dom', 'rep')), may hold values from 25 to 128, as said below
- node_perm: int32 [262144], P(('dom', 'rep')), may hold values from 0 to 262143, as said below
Outputs:
- grad_input: bfloat16 [262144, 512], P(('dom', 'rep'))
- weight_grad: float32 [512, 512], P('dom', 'rep')
Inputs may be any that keep to these rules, and one draw needn't show every extreme that they name: A node at input row i, held by device s = i // 1024, lands at node_perm[i] = t * 1024 + s * 4 + k with 0 <= k < 4; each device's rows cover every pair (t, k) exactly once, so every device passes exactly 4 rows to every device. `block_index`: first column below 64, second below 8; blocks may repeat. `block_count`: in each group of 8 devices along rep exactly one device has 128 live slots; the others have between 25 and 64.
All inputs are finite; a program needn't handle non-finite values.
Results may differ from a plain program's by a relative error of at most 0.005.
Values may be sent and summed in bfloat16 or wider, within the bound.
A program may use at most 64 MiB of HBM per device.

v0:
```python
import math

import jax
import jax.numpy as jnp
from jax import lax
from jax.sharding import PartitionSpec as P


def cut_along(x, dim, length):
    before, after = (x.shape[:dim], x.shape[dim + 1 :])
    return jnp.moveaxis(x.reshape(*before, length, -1, *after), dim, 0)


def in_order(parts, dim):
    parts = jnp.moveaxis(parts, 0, dim)
    shape = parts.shape
    return parts.reshape(*shape[:dim], shape[dim] * shape[dim + 1], *shape[dim + 2 :])


def one_exchange(x, axis, axes, splits, concats):
    sizes = [lax.axis_size(a) for a in axes]
    parts = cut_along(x, splits[0], sizes[0])
    parts = jnp.moveaxis(cut_along(parts, splits[1] + 1, sizes[1]), 0, 1)
    inside = parts.shape[2:]
    parts = parts.reshape(-1, *inside)
    parts = lax.all_to_all(parts, axis, split_axis=0, concat_axis=0, tiled=True)
    parts = in_order(parts.reshape(*sizes, *inside), concats[0] + 1)
    return in_order(parts, concats[1])


def sent_and_summed(x, axis, dim):
    parts = cut_along(x, dim, lax.axis_size(axis))
    arrived = lax.all_to_all(parts, axis, split_axis=0, concat_axis=0, tiled=True)
    return arrived.sum(axis=0)


def accumulate(running, block_values, index_values, live_count, stacked):
    group_len = 16
    turn_count = (live_count + group_len - 1) // group_len

    def add_group(turn_index, current):
        first_slot = turn_index * group_len
        block_part = lax.dynamic_slice_in_dim(block_values, first_slot, group_len, 0)
        index_part = lax.dynamic_slice_in_dim(index_values, first_slot, group_len, 0)
        alive_mask = first_slot + jnp.arange(group_len) < live_count
        source = jnp.take(stacked, index_part[:, 0], axis=0)
        products = jnp.einsum(
            "kij,kif->kjf", block_part, source, preferred_element_type=jnp.float32
        )
        targets = index_part[:, 1]
        onehot = jnp.where(
            alive_mask[:, None] & (targets[:, None] == jnp.arange(current.shape[0])[None, :]),
            1.0,
            0.0,
        ).astype(jnp.float32)
        return current + jnp.einsum(
            "kc,kjf->cjf",
            onehot,
            products,
            precision=lax.Precision.HIGHEST,
            preferred_element_type=jnp.float32,
        )

    return lax.fori_loop(0, turn_count, add_group, running)


def on_device(grad_out, features, weight, edge_blocks, block_index, block_count, node_perm):
    dom_count = lax.axis_size("dom")
    rep_count = lax.axis_size("rep")
    device_count = dom_count * rep_count
    row_count = grad_out.shape[0]
    feat_width = grad_out.shape[1]
    slot_rows = row_count // device_count
    block_side = edge_blocks.shape[1]
    col_blocks = row_count // block_side
    target_device = node_perm // row_count
    within_slot = node_perm % slot_rows
    target_slot = target_device * slot_rows + within_slot
    ordered = jnp.zeros_like(grad_out).at[target_slot].set(grad_out)
    ordered = ordered.reshape(dom_count, rep_count, slot_rows, feat_width)
    arrived = one_exchange(ordered, ("dom", "rep"), ("dom", "rep"), (0, 1), (0, 1))
    local_rows = arrived.reshape(row_count, feat_width)
    whole = lax.all_gather(local_rows, "rep", axis=0, tiled=True)
    stacked = whole.reshape(-1, block_side, feat_width)
    running = jnp.zeros((col_blocks, block_side, feat_width), jnp.float32)
    running = accumulate(running, edge_blocks, block_index, block_count[0], stacked)
    aggregated = running.reshape(row_count, feat_width).astype(jnp.bfloat16)
    grad_input = lax.dot_general(
        aggregated, weight, (((1,), (1,)), ((), ())), preferred_element_type=jnp.float32
    ).astype(jnp.bfloat16)
    scale_factor = 1.0 / math.sqrt(row_count * device_count)
    partial_rows = sent_and_summed(
        lax.dot_general(
            features, aggregated, (((0,), (0,)), ((), ())), preferred_element_type=jnp.float32
        )
        * scale_factor,
        "dom",
        0,
    )
    weight_grad = sent_and_summed(partial_rows, "rep", 1)
    return (grad_input, weight_grad)


def solution(mesh):
    in_specs = (
        P(("dom", "rep"), None),
        P(("dom", "rep"), None),
        P(),
        P(("dom", "rep"), None, None),
        P(("dom", "rep"), None),
        P(("dom", "rep")),
        P(("dom", "rep")),
    )
    out_specs = (P(("dom", "rep"), None), P("dom", "rep"))
    return jax.shard_map(
        on_device, mesh=mesh, in_specs=in_specs, out_specs=out_specs, check_vma=False
    )
```

profile of v0, /device:TPU:1, one launch (start us, length us, event | category | flops | bytes accessed | tf_op | source)
XLA Modules:
  0.0 271.5 jit_solution(8153901035986305665)
XLA Ops:
  7.2 0.8 compare_select_fusion.1
  8.0 5.8 %scatter_custom_fusion = bf16[1024,512]{1,0:T(8,128)(2,1)S(1)} fusion(s32[1024]{0:T(1024)S(1)} %compare_select_fusion.1, bf16[1024,512]{1,0:T(8,128)(2,1)} %param.9, bf16[]{:T(256)} %constant.78.clone.1), kind=kCustom, calls=%fused_computation.32 | custom fusion | bytes 1049088 | tf_op jit(solution)/shard_map/scatter | solution.py:79
  13.9 0.3 reshape_transpose_transpose_reshape_reshape_reshape.3
  14.1 45.9 %all_to_all.15 = bf16[256,1,1,4,512]{4,3,2,1,0:T(4,128)(2,1)S(1)} all-to-all(bf16[256,1,1,4,512]{4,3,2,1,0:T(4,128)(2,1)S(1)} %bitcast.38), channel_id=1, replica_groups=mesh['dom'=32,'rep'=8] {'dom','rep'}, dimensions={0} | all-to-all | bytes 2097152 | tf_op jit(solution)/shard_map/all_to_all | solution.py:26
  60.0 1.1 reshape_reshape.3
  61.8 46.9 %all-gather.2.cloned.1.call-done = bf16[8192,512]{1,0:T(8,128)(2,1)} async-done(((bf16[1024,512]{1,0:T(8,128)(2,1)}), bf16[8192,512]{1,0:T(8,128)(2,1)}) %all-gather.2.cloned.1.call-update) | async-done | bytes 8388624 | tf_op jit(solution)/shard_map/all_gather | solution.py:83
  108.7 1.7 broadcast_in_dim.29
  110.3 38.8 %while.10 = (s32[]{:T(128)}, f32[8,128,512]{2,0,1:T(8,128)}, s32[]{:T(128)}, s32[]{:T(128)}, s32[128,2]{0,1:T(2,128)S(1)}, /*index=5*/bf16[128,128,128]{2,1,0:T(...) while((s32[]{:T(128)}, f32[8,128,512]{2,0,1:T(8,128)}, ...), condition=%wide.region_2.3_spmd, body=%wide.region_1.2_spmd.sunk | while | flops 370673216 | bytes 19403756 | solution.py:64
  110.4 4.1 %gather_fusion = bf16[16,128,512]{2,1,0:T(8,128)(2,1)S(1)} fusion(bf16[64,128,512]{2,1,0:T(8,128)(2,1)} %get-tuple-element.147, s32[1024]{0:T(1024)S(1)} %pad_clamp_fusion.2), kind=kCustom, calls=%fused_computation.clone.1 | custom fusion | bytes 4194368 | tf_op jit(solution)/shard_map/while/body/jit(_take)/gather | solution.py:46
  114.5 1.8 fusion.44
  116.3 0.7 add_compare_fusion.2
  117.0 6.3 %fusion.45 = f32[8,128,512]{2,0,1:T(8,128)} fusion(f32[8,128,512]{2,0,1:T(8,128)} %get-tuple-element.131, f32[16,128,512]{2,1,0:T(8,128)S(1)} %fusion.44, s32[16]{0:T(128)S(1)} %get-tuple-element.118, pred[16]{0:T(512)(128)(4,1)S(1)} %add_compare_fusion.2), kind=kOutput, calls=%fused_computation.7.clone.1 | convolution fusion | flops 101187968 | bytes 8388688 | tf_op jit(solution)/shard_map/while/body/kc,kjf->cjf/dot_general | solution.py:56
  123.4 4.1 %gather_fusion = bf16[16,128,512]{2,1,0:T(8,128)(2,1)S(1)} fusion(bf16[64,128,512]{2,1,0:T(8,128)(2,1)} %get-tuple-element.147, s32[1024]{0:T(1024)S(1)} %pad_clamp_fusion.2), kind=kCustom, calls=%fused_computation.clone.1 | custom fusion | bytes 4194368 | tf_op jit(solution)/shard_map/while/body/jit(_take)/gather | solution.py:46
  127.4 1.8 fusion.44
  129.3 0.7 add_compare_fusion.2
  129.9 6.3 %fusion.45 = f32[8,128,512]{2,0,1:T(8,128)} fusion(f32[8,128,512]{2,0,1:T(8,128)} %get-tuple-element.131, f32[16,128,512]{2,1,0:T(8,128)S(1)} %fusion.44, s32[16]{0:T(128)S(1)} %get-tuple-element.118, pred[16]{0:T(512)(128)(4,1)S(1)} %add_compare_fusion.2), kind=kOutput, calls=%fused_computation.7.clone.1 | convolution fusion | flops 101187968 | bytes 8388688 | tf_op jit(solution)/shard_map/while/body/kc,kjf->cjf/dot_general | solution.py:56
  136.3 4.1 %gather_fusion = bf16[16,128,512]{2,1,0:T(8,128)(2,1)S(1)} fusion(bf16[64,128,512]{2,1,0:T(8,128)(2,1)} %get-tuple-element.147, s32[1024]{0:T(1024)S(1)} %pad_clamp_fusion.2), kind=kCustom, calls=%fused_computation.clone.1 | custom fusion | bytes 4194368 | tf_op jit(solution)/shard_map/while/body/jit(_take)/gather | solution.py:46
  140.4 1.8 fusion.44
  142.2 0.7 add_compare_fusion.2
  142.9 6.3 %fusion.45 = f32[8,128,512]{2,0,1:T(8,128)} fusion(f32[8,128,512]{2,0,1:T(8,128)} %get-tuple-element.131, f32[16,128,512]{2,1,0:T(8,128)S(1)} %fusion.44, s32[16]{0:T(128)S(1)} %get-tuple-element.118, pred[16]{0:T(512)(128)(4,1)S(1)} %add_compare_fusion.2), kind=kOutput, calls=%fused_computation.7.clone.1 | convolution fusion | flops 101187968 | bytes 8388688 | tf_op jit(solution)/shard_map/while/body/kc,kjf->cjf/dot_general | solution.py:56
  149.2 2.7 copy.25
  151.9 0.8 convolution_multiply_fusion
  152.6 100.8 %all_to_all.16 = f32[32,16,512]{2,1,0:T(8,128)S(1)} all-to-all(f32[32,16,512]{2,1,0:T(8,128)S(1)} %bitcast.42), channel_id=1, replica_groups=mesh['dom'=32,'rep'=8] {'dom'}, dimensions={0} | all-to-all | bytes 2097152 | tf_op jit(solution)/shard_map/all_to_all | solution.py:33
  253.5 0.1 reshape.34
  253.6 0.7 reshape.55
  254.3 3.6 %all-to-all-start.2 = ((f32[8,1,1024]{2,1,0:T(1,128)}), f32[8,1,1024]{2,1,0:T(1,128)S(1)}, u32[]{:S(2)}, u32[]{:S(2)}) async-start(f32[8,1,1024]{2,1,0:T(1,128)} %reshape.55), calls=%async_computation.2 | async-start | bytes 65536 | tf_op jit(solution)/shard_map/all_to_all | solution.py:33
  258.0 2.8 %convolution_convert_fusion = bf16[1024,512]{1,0:T(8,128)(2,1)} fusion(bf16[1024,512]{1,0:T(8,128)(2,1)S(1)} %bitcast.41, bf16[512,512]{1,0:T(8,128)(2,1)} %param.11), kind=kOutput, calls=%fused_computation.30 | convolution fusion | flops 537395200 | bytes 2621440 | tf_op jit(solution)/shard_map/dot_general | solution.py:88
  260.7 2.0 all-to-all-done.2
  262.7 0.5 broadcast.48
  263.2 0.7 reduce
  263.9 0.1 reshape.56
  264.0 0.6 reduce_sum.19
  (20 shorter events, 0.4 us)
Async XLA Ops:
  7.2 144.7 %copy-start = (bf16[1024,512]{1,0:T(8,128)(2,1)S(1)}, bf16[1024,512]{1,0:T(8,128)(2,1)}, u32[]{:S(2)}) copy-start(bf16[1024,512]{1,0:T(8,128)(2,1)} %param.10) | copy-start | bytes 3145732
  7.2 101.5 %all-gather.2.cloned.1.call-start = ((), (), s32[]{:S(2)}) async-start(), calls=%async_computation.3 | async-start | bytes 9437184 | tf_op jit(solution)/shard_map/all_gather | solution.py:83
  61.1 49.2 %copy-start.1 = (s32[128,2]{0,1:T(2,128)S(1)}, s32[128,2]{0,1:T(2,128)}, u32[]{:S(2)}) copy-start(s32[128,2]{0,1:T(2,128)} %param.13) | copy-start | bytes 3076
  254.3 8.4 %all-to-all-start.2 = ((f32[8,1,1024]{2,1,0:T(1,128)}), f32[8,1,1024]{2,1,0:T(1,128)S(1)}, u32[]{:S(2)}, u32[]{:S(2)}) async-start(f32[8,1,1024]{2,1,0:T(1,128)} %reshape.55), calls=%async_computation.2 | async-start | bytes 65536 | tf_op jit(solution)/shard_map/all_to_all | solution.py:33
Sparse Core Ops, SparseCore 0:
  61.2 47.3 all-gather.1
where the time goes:
time: 273 us; the launch traced here: 271 us
  blocking collectives  147 us (54%)
  waiting for transfers between devices  48.9 us (18%)
  matrix products  27.8 us (10%)
  local copies, waits for them, and re-layouts  25.4 us (9%)
  between operations  14.8 us (5%)
  other arithmetic  4.21 us (2%)
  starting transfers between devices  3.67 us (1%)
    all_to_all x1, blocking collectives, sent_and_summed(): lax.all_to_all(parts, axis, split_axis=0, concat_axis=0, tiled=True)  101 us
    all_gather x1, waiting for transfers between devices, on_device(): whole = lax.all_gather(local_rows, 'rep', axis=0, tiled=True)  46.9 us
    all_to_all x1, blocking collectives, one_exchange(): parts = lax.all_to_all(parts, axis, split_axis=0, concat_axis=0, tiled=True)  45.9 us
    dot_general x3, matrix products, add_group(): jnp.einsum('kc,kjf->cjf', onehot, products, precision=lax.Precision.HIGHE...  18.8 us
    gather x3, local copies, waits for them, and re-layouts, add_group(): source = jnp.take(stacked, index_part[:, 0], axis=0)  12.2 us
    scatter x1, local copies, waits for them, and re-layouts, on_device(): ordered = jnp.zeros_like(grad_out).at[target_slot].set(grad_out)  5.84 us
    dot_general x3, matrix products, add_group(): jnp.einsum('kij,kif->kjf', block_part, source, preferred_element_type=jnp...  5.49 us
  transfers between devices with their start and end apart: 2, of which 2 were waited for; matrix products, arithmetic and copies ran while one was open for 1% of the time, Pallas kernels for 0%

commit v1 on v0

v1 whole, which is shorter than its diff:
```python
import math

import jax
import jax.numpy as jnp
from jax import lax
from jax.experimental import pallas as pl
from jax.experimental.pallas import tpu as pltpu
from jax.sharding import PartitionSpec as P


def cut_along(x, dim, length):
    before, after = (x.shape[:dim], x.shape[dim + 1 :])
    return jnp.moveaxis(x.reshape(*before, length, -1, *after), dim, 0)


def in_order(parts, dim):
    parts = jnp.moveaxis(parts, 0, dim)
    shape = parts.shape
    return parts.reshape(*shape[:dim], shape[dim] * shape[dim + 1], *shape[dim + 2 :])


def one_exchange(x, axis, axes, splits, concats):
    sizes = [lax.axis_size(a) for a in axes]
    parts = cut_along(x, splits[0], sizes[0])
    parts = jnp.moveaxis(cut_along(parts, splits[1] + 1, sizes[1]), 0, 1)
    inside = parts.shape[2:]
    parts = parts.reshape(-1, *inside)
    parts = lax.all_to_all(parts, axis, split_axis=0, concat_axis=0, tiled=True)
    parts = in_order(parts.reshape(*sizes, *inside), concats[0] + 1)
    return in_order(parts, concats[1])


def sent_and_summed(x, axis, dim):
    parts = cut_along(x, dim, lax.axis_size(axis))
    arrived = lax.all_to_all(parts, axis, split_axis=0, concat_axis=0, tiled=True)
    return arrived.sum(axis=0)


def slots_kernel(scale, index_ref, count_ref, src_ref, edge_ref, feat_ref, weight_ref,
                 gi_ref, wg_ref, acc_ref):
    acc_ref[...] = jnp.zeros_like(acc_ref)

    @pl.loop(0, count_ref[0])
    def _(s):
        b = index_ref[2 * s]
        c = index_ref[2 * s + 1]
        acc_ref[c] += lax.dot_general(
            edge_ref[s], src_ref[b], (((0,), (0,)), ((), ())),
            preferred_element_type=jnp.float32)

    side = acc_ref.shape[1]

    @pl.loop(0, acc_ref.shape[0])
    def _(c):
        rows = pl.ds(pl.multiple_of(c * side, side), side)
        agg = acc_ref[c].astype(jnp.bfloat16)
        gi_ref[rows, :] = lax.dot_general(
            agg, weight_ref[...], (((1,), (1,)), ((), ())),
            preferred_element_type=jnp.float32).astype(gi_ref.dtype)
        part = lax.dot_general(
            feat_ref[rows, :], agg, (((0,), (0,)), ((), ())),
            preferred_element_type=jnp.float32)

        @pl.when(c == 0)
        def _():
            wg_ref[...] = part

        @pl.when(c > 0)
        def _():
            wg_ref[...] += part

    wg_ref[...] = wg_ref[...] * scale


def slots(scale, index, count, src, edge, feat, weight):
    rows, width = feat.shape
    side = edge.shape[1]
    smem = pl.BlockSpec(memory_space=pltpu.SMEM)
    vmem = pl.BlockSpec(memory_space=pltpu.VMEM)
    return pl.pallas_call(
        lambda *refs: slots_kernel(scale, *refs),
        out_shape=(jax.ShapeDtypeStruct((rows, weight.shape[0]), jnp.bfloat16),
                   jax.ShapeDtypeStruct((width, src.shape[2]), jnp.float32)),
        in_specs=[smem, smem, vmem, vmem, vmem, vmem],
        out_specs=(vmem, vmem),
        scratch_shapes=[pltpu.VMEM((rows // side, side, src.shape[2]), jnp.float32)],
        compiler_params=pltpu.CompilerParams(vmem_limit_bytes=40 << 20),
        name="slots",
    )(index.reshape(-1), count, src, edge, feat, weight)


def on_device(grad_out, features, weight, edge_blocks, block_index, block_count, node_perm):
    dom_count = lax.axis_size("dom")
    rep_count = lax.axis_size("rep")
    device_count = dom_count * rep_count
    row_count = grad_out.shape[0]
    feat_width = grad_out.shape[1]
    slot_rows = row_count // device_count
    block_side = edge_blocks.shape[1]
    target_device = node_perm // row_count
    within_slot = node_perm % slot_rows
    target_slot = target_device * slot_rows + within_slot
    onehot = (jnp.arange(row_count)[:, None] == target_slot[None, :]).astype(jnp.bfloat16)
    ordered = jnp.dot(onehot, grad_out, preferred_element_type=jnp.float32).astype(jnp.bfloat16)
    ordered = ordered.reshape(dom_count, rep_count, slot_rows, feat_width)
    arrived = one_exchange(ordered, ("dom", "rep"), ("dom", "rep"), (0, 1), (0, 1))
    local_rows = arrived.reshape(row_count, feat_width)
    whole = lax.all_gather(local_rows, "rep", axis=0, tiled=True)
    stacked = whole.reshape(-1, block_side, feat_width)
    scale_factor = 1.0 / math.sqrt(row_count * device_count)
    grad_input, partial = slots(
        scale_factor, block_index, block_count, stacked, edge_blocks, features, weight)
    partial_cols = sent_and_summed(partial, "rep", 1)
    weight_grad = sent_and_summed(partial_cols, "dom", 0)
    return (grad_input, weight_grad)


def solution(mesh):
    in_specs = (
        P(("dom", "rep"), None),
        P(("dom", "rep"), None),
        P(),
        P(("dom", "rep"), None, None),
        P(("dom", "rep"), None),
        P(("dom", "rep")),
        P(("dom", "rep")),
    )
    out_specs = (P(("dom", "rep"), None), P("dom", "rep"))
    return jax.shard_map(
        on_device, mesh=mesh, in_specs=in_specs, out_specs=out_specs, check_vma=False
    )
```

time: 273 us -> 193 us (0.71)
  blocking collectives: 147 us -> 96.2 us
  matrix products: 27.8 us -> 2.22 us
  Pallas kernels: 0 us -> 21.3 us
  local copies, waits for them, and re-layouts: 25.4 us -> 8.72 us
  starting transfers between devices: 3.67 us -> 0.04 us
    all_to_all x1 -> x2, blocking collectives: 101 us -> 50.3 us  [sent_and_summed(): lax.all_to_all(parts, axis, split_axis=0, concat_axis=0, tiled=True)]
    dot_general x8 -> x1, matrix products: 27.8 us -> 2.22 us  [on_device(): jnp.dot(onehot, grad_out, preferred_element_type=jnp.float32)]
    pallas_call x0 -> x1, Pallas kernels: none -> 21.3 us  [slots(): pl.pallas_call(lambda *refs: slots_kernel(scale, *refs), out_shape=(jax.S...]
    gather x3 -> x0, local copies, waits for them, and re-layouts: 12.2 us -> none  [add_group(): source = jnp.take(stacked, index_part[:, 0], axis=0)]
    scatter x1 -> x0, local copies, waits for them, and re-layouts: 5.84 us -> none  [on_device(): ordered = jnp.zeros_like(grad_out).at[target_slot].set(grad_out)]
    all_to_all x1 -> x0, starting transfers between devices: 3.63 us -> none  [sent_and_summed(): lax.all_to_all(parts, axis, split_axis=0, concat_axis=0, tiled=True)]
    unnamed x6 -> x13, local copies, waits for them, and re-layouts: 0.79 us -> 4.05 us
  transfers between devices with their start and end apart: 2 -> 1, of which waited for: 2 -> 1; matrix products, arithmetic and copies ran while one was open for 1% -> 0% of each run, Pallas kernels for 0% -> 0%
where the time goes in v1:
time: 193 us; the launch traced here: 192 us
  blocking collectives  96.2 us (50%)
  waiting for transfers between devices  46.6 us (24%)
  Pallas kernels  21.3 us (11%)
  between operations  14.8 us (8%)
  local copies, waits for them, and re-layouts  8.72 us (5%)
  other arithmetic  2.44 us (1%)
  matrix products  2.22 us (1%)
    all_to_all x2, blocking collectives, sent_and_summed(): lax.all_to_all(parts, axis, split_axis=0, concat_axis=0, tiled=True)  50.3 us
    all_gather x1, waiting for transfers between devices, on_device(): whole = lax.all_gather(local_rows, 'rep', axis=0, tiled=True)  46.6 us
    all_to_all x1, blocking collectives, one_exchange(): parts = lax.all_to_all(parts, axis, split_axis=0, concat_axis=0, tiled=True)  46 us
    pallas_call x1, Pallas kernels, slots(): pl.pallas_call(lambda *refs: slots_kernel(scale, *refs), out_shape=(jax.S...  21.3 us
    unnamed x13, local copies, waits for them, and re-layouts  4.05 us
  transfers between devices with their start and end apart: 1, of which 1 were waited for; matrix products, arithmetic and copies ran while one was open for 0% of the time, Pallas kernels for 0%

profile of v1, /device:TPU:1, one launch (start us, length us, event | category | flops | bytes accessed | tf_op | source)
XLA Modules:
  0.0 192.3 jit_solution(16882170775036300027)
XLA Ops:
  7.2 0.0 copy-start
  7.2 0.0 all-gather.2.cloned.1.call-start
  7.2 0.8 fusion.5
  8.0 0.4 copy-done
  8.4 2.2 %fusion.2 = bf16[1024,512]{1,0:T(8,128)(2,1)} fusion(bf16[1024,512]{1,0:T(8,128)(2,1)S(1)} %copy-done, s32[1024]{0:T(1024)S(1)} %fusion.5), kind=kOutput, calls=%fused_computation.3 | convolution fusion | flops 1075314688 | bytes 2101248 | tf_op jit(solution)/shard_map/dot_general | solution.py:104
  10.6 0.0 copy-start.4
  10.6 0.0 copy-start.2
  10.6 1.4 reshape_transpose_transpose_reshape_reshape_reshape.3
  12.1 46.0 %all_to_all.15 = bf16[256,1,1,4,512]{4,3,2,1,0:T(4,128)(2,1)} all-to-all(bf16[256,1,1,4,512]{4,3,2,1,0:T(4,128)(2,1)S(1)} %bitcast.17), channel_id=1, replica_groups=mesh['dom'=32,'rep'=8] {'dom','rep'}, dimensions={0} | all-to-all | bytes 2097152 | tf_op jit(solution)/shard_map/all_to_all | solution.py:28
  58.0 2.1 %reshape_reshape.3 = bf16[1024,512]{1,0:T(8,128)(2,1)} reshape(bf16[32,8,1,4,512]{4,3,1,0,2:T(4,128)(2,1)} %bitcast.18) | data formatting | bytes 2097152 | tf_op jit(solution)/shard_map/reshape;reshape | solution.py:107
  60.2 0.0 all-gather.2.cloned.1.call-update
  60.2 0.0 copy-done.4
  60.2 0.1 copy.14
  60.3 0.1 reshape.23.refs_0_
  61.1 46.6 %all-gather.2.cloned.1.call-done = bf16[8192,512]{1,0:T(8,128)(2,1)} async-done(((bf16[1024,512]{1,0:T(8,128)(2,1)}), bf16[8192,512]{1,0:T(8,128)(2,1)}) %all-gather.2.cloned.1.call-update) | async-done | bytes 8388624 | tf_op jit(solution)/shard_map/all_gather | solution.py:108
  107.7 0.0 copy-done.2
  107.7 0.0 copy-start.1
  107.7 2.2 %copy-done.1 = bf16[128,128,128]{2,1,0:T(8,128)(2,1)S(1)} copy-done((bf16[128,128,128]{2,1,0:T(8,128)(2,1)S(1)}, bf16[128,128,128]{2,1,0:T(8,128)(2,1)}, u32[]{:S(2)}) %copy-start.1) | copy-done | bytes 4194328
  109.9 0.0 copy-start.3
  109.9 1.0 copy-done.3
  111.0 21.3 %slots.1 = (bf16[1024,512]{1,0:T(8,128)(2,1)}, f32[512,512]{1,0:T(8,128)S(1)}) custom-call(s32[256]{0:T(256)S(1)} %reshape.23.refs_0_, s32[1]{0:T(128)S(6)} %copy.18.refs_1_, bf16[64,128,512]{2,1,0:T(8,128)(2,1)} %bitcast.16, bf16[128,128,128]{2,1,0:T(8,128)(2,1)S(1)} %copy-done.1, bf16[1024,512]{1,0:T(8,128)(2,1)S(1)} %copy-done.2, ...), custom_call_target="tpu_custom_call" | custom-call | tf_op jit(solution)/shard_map/slots/pallas_call | solution.py:80
  132.3 0.3 copy.16
  132.6 31.3 %all_to_all.16 = f32[8,512,64]{1,2,0:T(8,128)S(1)} all-to-all(f32[8,512,64]{1,2,0:T(8,128)S(1)} %bitcast.19), channel_id=1, replica_groups=mesh['dom'=32,'rep'=8] {'rep'}, dimensions={0} | all-to-all | bytes 2097152 | tf_op jit(solution)/shard_map/all_to_all | solution.py:35
  163.9 0.1 reduce_sum.18
  164.0 0.1 copy.17
  164.2 0.2 reshape.29
  164.3 18.9 %all_to_all.17 = f32[32,1,1024]{2,1,0:T(1,128)S(1)} all-to-all(f32[32,1,1024]{2,1,0:T(1,128)S(1)} %reshape.29), channel_id=1, replica_groups=mesh['dom'=32,'rep'=8] {'dom'}, dimensions={0} | all-to-all | bytes 262144 | tf_op jit(solution)/shard_map/all_to_all | solution.py:35
  183.3 0.5 broadcast.14
  183.8 0.9 reduce
  184.8 0.1 reshape.30
  184.9 0.6 reduce_sum.19
Async XLA Ops:
  7.2 1.2 copy-start
  7.2 100.6 %all-gather.2.cloned.1.call-start = ((), (), s32[]{:S(2)}) async-start(), calls=%async_computation.3 | async-start | bytes 9437184 | tf_op jit(solution)/shard_map/all_gather | solution.py:108
  10.6 49.6 %copy-start.4 = (s32[128,2]{0,1:T(2,128)S(1)}, s32[128,2]{0,1:T(2,128)}, u32[]{:S(2)}) copy-start(s32[128,2]{0,1:T(2,128)} %param.11) | copy-start | bytes 3076
  10.6 97.1 %copy-start.2 = (bf16[1024,512]{1,0:T(8,128)(2,1)S(1)}, bf16[1024,512]{1,0:T(8,128)(2,1)}, u32[]{:S(2)}) copy-start(bf16[1024,512]{1,0:T(8,128)(2,1)} %refs_4_.1) | copy-start | bytes 3145732
  107.7 2.2 %copy-start.1 = (bf16[128,128,128]{2,1,0:T(8,128)(2,1)S(1)}, bf16[128,128,128]{2,1,0:T(8,128)(2,1)}, u32[]{:S(2)}) copy-start(bf16[128,128,128]{2,1,0:T(8,128)(2,1)} %refs_3_.1) | copy-start | bytes 12582916
  109.9 1.0 copy-start.3
Sparse Core Ops, SparseCore 0:
  60.3 47.3 all-gather.1

commit v2 on v1

v2 whole, which is shorter than its diff:
```python
import math

import jax
import jax.numpy as jnp
from jax import lax
from jax.experimental import pallas as pl
from jax.experimental.pallas import tpu as pltpu
from jax.sharding import PartitionSpec as P


def slots_kernel(scale, index_ref, count_ref, src_ref, edge_ref, feat_ref, weight_ref,
                 gi_ref, wg_ref, acc_ref):
    acc_ref[...] = jnp.zeros_like(acc_ref)

    @pl.loop(0, count_ref[0])
    def _(s):
        b = index_ref[2 * s]
        c = index_ref[2 * s + 1]
        acc_ref[c] += lax.dot_general(
            edge_ref[s], src_ref[b], (((0,), (0,)), ((), ())),
            preferred_element_type=jnp.float32)

    side = acc_ref.shape[1]

    @pl.loop(0, acc_ref.shape[0])
    def _(c):
        rows = pl.ds(pl.multiple_of(c * side, side), side)
        agg = acc_ref[c].astype(jnp.bfloat16)
        gi_ref[rows, :] = lax.dot_general(
            agg, weight_ref[...], (((1,), (1,)), ((), ())),
            preferred_element_type=jnp.float32).astype(gi_ref.dtype)
        part = lax.dot_general(
            feat_ref[rows, :], agg, (((0,), (0,)), ((), ())),
            preferred_element_type=jnp.float32)

        @pl.when(c == 0)
        def _():
            wg_ref[...] = part

        @pl.when(c > 0)
        def _():
            wg_ref[...] += part

    wg_ref[...] = wg_ref[...] * scale


def slots(scale, index, count, src, edge, feat, weight):
    rows, width = feat.shape
    side = edge.shape[1]
    smem = pl.BlockSpec(memory_space=pltpu.SMEM)
    vmem = pl.BlockSpec(memory_space=pltpu.VMEM)
    return pl.pallas_call(
        lambda *refs: slots_kernel(scale, *refs),
        out_shape=(jax.ShapeDtypeStruct((rows, weight.shape[0]), jnp.bfloat16),
                   jax.ShapeDtypeStruct((width, src.shape[2]), jnp.float32)),
        in_specs=[smem, smem, vmem, vmem, vmem, vmem],
        out_specs=(vmem, vmem),
        scratch_shapes=[pltpu.VMEM((rows // side, side, src.shape[2]), jnp.float32)],
        compiler_params=pltpu.CompilerParams(vmem_limit_bytes=40 << 20),
        name="slots",
    )(index.reshape(-1), count, src, edge, feat, weight)


MESH = pl.DeviceIdType.MESH


def wrap(value, size):
    return lax.rem(value + 2 * size, size)


def regroup_kernel(zs_n, xs_n, ys_n, perm_ref, grad_ref, out_ref, ordered, raw, unperm,
                   own_sem, a_send, a_recv, y_send, y_recv, f_send, f_recv, p_send, p_recv):
    d = lax.axis_index("dom")
    r = lax.axis_index("rep")
    z, x = d // xs_n, lax.rem(d, xs_n)
    y, c = r // 2, lax.rem(r, 2)
    peers = zs_n * xs_n
    slot_rows = 4
    piece = 2 * ys_n * slot_rows
    r_up = wrap(y + 1, ys_n) * 2 + c
    r_down = wrap(y - 1, ys_n) * 2 + c
    r_far = wrap(y + 2, ys_n) * 2 + c
    r_pair = r + 1 - 2 * c

    def offset(j):
        return ((j + 1) // 2) * (2 * lax.rem(j, 2) - 1)

    barrier = pltpu.get_barrier_semaphore()

    @pl.loop(1, peers)
    def _(n):
        pl.semaphore_signal(barrier, inc=1, device_id={"dom": wrap(d + n, peers), "rep": r},
                            device_id_type=MESH)

    for other in (r_up, r_down, r_pair):
        pl.semaphore_signal(barrier, inc=1, device_id={"dom": d, "rep": other},
                            device_id_type=MESH)

    perm = perm_ref[...]
    target = (perm // grad_ref.shape[0]) * slot_rows + lax.rem(perm, slot_rows)
    tile = 256

    @pl.loop(0, grad_ref.shape[0] // tile)
    def _(t):
        rows = lax.broadcasted_iota(jnp.int32, (tile, grad_ref.shape[0]), 0) + t * tile
        hot = jnp.where(rows == target, 1.0, 0.0).astype(jnp.bfloat16)
        ordered[pl.ds(pl.multiple_of(t * tile, tile), tile), :] = lax.dot_general(
            hot, grad_ref[...], (((1,), (0,)), ((), ())),
            preferred_element_type=jnp.float32).astype(jnp.bfloat16)

    q = lax.broadcasted_iota(jnp.int32, (tile, tile), 0)
    p = lax.broadcasted_iota(jnp.int32, (tile, tile), 1)
    wanted = lax.rem(q // slot_rows, 8) * piece + (q // piece) * slot_rows + lax.rem(q, slot_rows)
    unperm[...] = jnp.where(p == wanted, 1.0, 0.0).astype(jnp.bfloat16)

    pl.semaphore_wait(barrier, peers - 1 + 3)

    own = pltpu.make_async_copy(
        ordered.at[pl.ds(pl.multiple_of(d * piece, piece), piece)], raw.at[z, x, r], own_sem)
    own.start()

    def a_copy(n, zs, xs):
        j, i = n // xs_n, lax.rem(n, xs_n)
        to = wrap(z + offset(j), zs_n) * xs_n + wrap(x + i, xs_n)
        return pltpu.make_async_remote_copy(
            src_ref=ordered.at[pl.ds(pl.multiple_of(to * piece, piece), piece)],
            dst_ref=raw.at[zs, xs, r],
            send_sem=a_send.at[n], recv_sem=a_recv.at[n],
            device_id={"dom": to, "rep": r}, device_id_type=MESH)

    @pl.loop(1, peers)
    def _(n):
        a_copy(n, z, x).start()

    def chunk_of(j):
        return wrap(z - offset(j), zs_n)

    def y_copy(j, way, owner):
        part = raw.at[chunk_of(j), :, owner]
        return pltpu.make_async_remote_copy(
            src_ref=part, dst_ref=part, send_sem=y_send.at[way, j], recv_sem=y_recv.at[way, j],
            device_id={"dom": d, "rep": (r_up, r_down)[way]}, device_id_type=MESH)

    half = xs_n // 2

    def f_copy(j, way, owner):
        part = raw.at[chunk_of(j), pl.ds(way * half, half), owner]
        return pltpu.make_async_remote_copy(
            src_ref=part, dst_ref=part, send_sem=f_send.at[way, j], recv_sem=f_recv.at[way, j],
            device_id={"dom": d, "rep": (r_up, r_down)[way]}, device_id_type=MESH)

    def p_copy(j, which, owner):
        part = raw.at[chunk_of(j), :, owner]
        return pltpu.make_async_remote_copy(
            src_ref=part, dst_ref=part, send_sem=p_send.at[which, j],
            recv_sem=p_recv.at[which, j],
            device_id={"dom": d, "rep": r_pair}, device_id_type=MESH)

    @pl.loop(0, zs_n + 3)
    def _(step):
        @pl.when(step < zs_n)
        def _():
            j = step

            @pl.when(j == 0)
            def _():
                own.wait()

            @pl.loop(0, xs_n)
            def _(i):
                @pl.when(j * xs_n + i > 0)
                def _():
                    a_copy(j * xs_n + i, chunk_of(j), wrap(x - i, xs_n)).wait_recv()

            y_copy(j, 0, r).start()
            y_copy(j, 1, r).start()
            p_copy(j, 0, r).start()

        @pl.when((step >= 1) & (step < zs_n + 1))
        def _():
            j = step - 1
            y_copy(j, 0, r_down).wait_recv()
            f_copy(j, 0, r_down).start()
            p_copy(j, 1, r_down).start()
            y_copy(j, 1, r_up).wait_recv()
            f_copy(j, 1, r_up).start()
            p_copy(j, 2, r_up).start()

        @pl.when((step >= 2) & (step < zs_n + 2))
        def _():
            j = step - 2
            f_copy(j, 0, r_far).wait_recv()
            f_copy(j, 1, r_far).wait_recv()
            p_copy(j, 3, r_far).start()

        @pl.when(step >= 3)
        def _():
            j = step - 3
            zs = chunk_of(j)
            flip = 1 - 2 * c
            p_copy(j, 0, r + flip).wait_recv()
            p_copy(j, 1, r_down + flip).wait_recv()
            p_copy(j, 2, r_up + flip).wait_recv()
            p_copy(j, 3, r_far + flip).wait_recv()
            for xs in range(xs_n):
                rows = raw[zs, xs].reshape(tile, out_ref.shape[-1])
                placed = lax.dot_general(
                    unperm[...], rows, (((1,), (0,)), ((), ())),
                    preferred_element_type=jnp.float32).astype(jnp.bfloat16)
                for t in range(2 * ys_n):
                    out_ref[t, zs, xs * piece:(xs + 1) * piece, :] = placed[
                        t * piece:(t + 1) * piece, :]

    @pl.loop(1, peers)
    def _(n):
        a_copy(n, z, x).wait_send()

    @pl.loop(0, zs_n)
    def _(j):
        for way in range(2):
            y_copy(j, way, r).wait_send()
            f_copy(j, way, r).wait_send()
        for which in range(4):
            p_copy(j, which, r).wait_send()


def regroup(perm, grad, sizes):
    zs_n, xs_n, ys_n = sizes
    rows, width = grad.shape
    reps, doms = 2 * ys_n, zs_n * xs_n
    piece = rows // doms
    vmem = pl.BlockSpec(memory_space=pltpu.VMEM)
    dma = pltpu.SemaphoreType.DMA
    return pl.pallas_call(
        lambda *refs: regroup_kernel(zs_n, xs_n, ys_n, *refs),
        out_shape=jax.ShapeDtypeStruct((reps, zs_n, rows // zs_n, width), grad.dtype),
        in_specs=[vmem, vmem],
        out_specs=vmem,
        scratch_shapes=[
            pltpu.VMEM((rows, width), grad.dtype),
            pltpu.VMEM((zs_n, xs_n, reps, piece, width), grad.dtype),
            pltpu.VMEM((256, 256), grad.dtype),
            dma, dma((doms,)), dma((doms,)),
            dma((2, zs_n)), dma((2, zs_n)), dma((2, zs_n)), dma((2, zs_n)),
            dma((4, zs_n)), dma((4, zs_n)),
        ],
        compiler_params=pltpu.CompilerParams(
            collective_id=0, has_side_effects=True, vmem_limit_bytes=32 << 20),
        name="regroup",
    )(perm.reshape(1, rows), grad)


def reduce_kernel(zs_n, xs_n, ys_n, part_ref, out_ref, pair_in, y_in, half_sum, cols_sum, dom_in,
                  result, c_send, c_recv, y_send, y_recv, d_send, d_recv, l_send, l_recv):
    d = lax.axis_index("dom")
    r = lax.axis_index("rep")
    y, c = r // 2, lax.rem(r, 2)
    doms = zs_n * xs_n
    group = doms // 2
    rows = out_ref.shape[0]
    lanes = 2 * out_ref.shape[1]
    tall = group * rows
    r_pair = r + 1 - 2 * c
    takes = d // group == c
    barrier = pltpu.get_barrier_semaphore()

    @pl.when(takes)
    def _():
        @pl.loop(1, doms)
        def _(n):
            pl.semaphore_signal(barrier, inc=1, device_id={"dom": wrap(d + n, doms), "rep": r},
                                device_id_type=MESH)

    @pl.loop(1, ys_n)
    def _(n):
        pl.semaphore_signal(barrier, inc=1,
                            device_id={"dom": d, "rep": wrap(y + n, ys_n) * 2 + c},
                            device_id_type=MESH)

    pl.semaphore_signal(barrier, inc=1, device_id={"dom": d, "rep": r_pair}, device_id_type=MESH)

    @pl.when(takes)
    def _():
        pl.semaphore_wait(barrier, group - 1 + ys_n)

    @pl.when(jnp.logical_not(takes))
    def _():
        pl.semaphore_wait(barrier, group + ys_n)

    def wide(n):
        return pl.ds(pl.multiple_of(wrap(y + n, ys_n) * lanes, lanes), lanes)

    order = (2, 1, 3, 0)
    mine = pl.ds(pl.multiple_of(c * tall, tall), tall)
    other = pl.ds(pl.multiple_of((1 - c) * tall, tall), tall)

    def c_copy(n):
        return pltpu.make_async_remote_copy(
            src_ref=part_ref.at[other, wide(n)], dst_ref=pair_in.at[n],
            send_sem=c_send.at[n], recv_sem=c_recv.at[n],
            device_id={"dom": d, "rep": r_pair}, device_id_type=MESH)

    def y_copy(n):
        return pltpu.make_async_remote_copy(
            src_ref=half_sum.at[n], dst_ref=y_in.at[n],
            send_sem=y_send.at[n], recv_sem=y_recv.at[n],
            device_id={"dom": d, "rep": wrap(y + n, ys_n) * 2 + c}, device_id_type=MESH)

    for n in order:
        c_copy(n).start()
    for n in order:
        c_copy(n).wait_recv()
        half_sum[n] = part_ref[mine, wide(n)] + pair_in[n]
        if n:
            y_copy(n).start()
    for n in (1, 3, 2):
        y_copy(n).wait_recv()
    cols_sum[...] = (half_sum[0] + y_in[1]) + (y_in[2] + y_in[3])

    def d_copy(n):
        return pltpu.make_async_remote_copy(
            src_ref=cols_sum.at[pl.ds(pl.multiple_of(n * rows, rows), rows)],
            dst_ref=dom_in.at[d],
            send_sem=d_send.at[n], recv_sem=d_recv.at[d],
            device_id={"dom": c * group + n, "rep": r}, device_id_type=MESH)

    @pl.loop(0, group)
    def _(m):
        n = lax.rem(m + d, group)

        @pl.when(c * group + n != d)
        def _():
            d_copy(n).start()

    def l_copy():
        return pltpu.make_async_remote_copy(
            src_ref=result, dst_ref=result, send_sem=l_send, recv_sem=l_recv,
            device_id={"dom": d, "rep": r_pair}, device_id_type=MESH)

    @pl.when(takes)
    def _():
        dom_in[d] = cols_sum[pl.ds(pl.multiple_of((d - c * group) * rows, rows), rows), :]

        @pl.loop(0, doms)
        def _(s):
            @pl.when(s != d)
            def _():
                pltpu.make_async_remote_copy(
                    src_ref=cols_sum.at[pl.ds(0, rows)], dst_ref=dom_in.at[s],
                    send_sem=d_send.at[0], recv_sem=d_recv.at[s],
                    device_id={"dom": d, "rep": r_pair}, device_id_type=MESH).wait_recv()

        total = dom_in[0]
        for s in range(1, doms):
            total = total + dom_in[s]
        result[...] = total
        l_copy().start()
        l_copy().wait_send()

    @pl.when(jnp.logical_not(takes))
    def _():
        l_copy().wait_recv()

    got = result[...]
    out_ref[...] = jnp.where(c == 0, got[:, : lanes // 2], got[:, lanes // 2 :])

    for n in order:
        c_copy(n).wait_send()
        if n:
            y_copy(n).wait_send()

    @pl.loop(0, group)
    def _(n):
        @pl.when(c * group + n != d)
        def _():
            d_copy(n).wait_send()


def reduce_parts(part, sizes):
    zs_n, xs_n, ys_n = sizes
    rows, cols = part.shape
    doms = zs_n * xs_n
    tall, lanes = rows // 2, cols // ys_n
    vmem = pl.BlockSpec(memory_space=pltpu.VMEM)
    dma = pltpu.SemaphoreType.DMA
    f32 = jnp.float32
    return pl.pallas_call(
        lambda *refs: reduce_kernel(zs_n, xs_n, ys_n, *refs),
        out_shape=jax.ShapeDtypeStruct((rows // doms, lanes // 2), f32),
        in_specs=[vmem],
        out_specs=vmem,
        scratch_shapes=[
            pltpu.VMEM((ys_n, tall, lanes), f32), pltpu.VMEM((ys_n, tall, lanes), f32),
            pltpu.VMEM((ys_n, tall, lanes), f32), pltpu.VMEM((tall, lanes), f32),
            pltpu.VMEM((doms, rows // doms, lanes), f32), pltpu.VMEM((rows // doms, lanes), f32),
            dma((ys_n,)), dma((ys_n,)), dma((ys_n,)), dma((ys_n,)),
            dma((doms // 2,)), dma((doms,)), dma, dma,
        ],
        compiler_params=pltpu.CompilerParams(collective_id=1, has_side_effects=True),
        name="reduce",
    )(part)


SIZES = (8, 4, 4)


def on_device(grad_out, features, weight, edge_blocks, block_index, block_count, node_perm):
    block_side = edge_blocks.shape[1]
    stacked = regroup(node_perm, grad_out, SIZES).reshape(-1, block_side, grad_out.shape[1])
    nodes = grad_out.shape[0] * lax.axis_size("dom") * lax.axis_size("rep")
    grad_input, partial = slots(
        1.0 / math.sqrt(nodes), block_index, block_count, stacked, edge_blocks, features, weight)
    return (grad_input, reduce_parts(partial, SIZES))


def solution(mesh):
    in_specs = (
        P(("dom", "rep"), None),
        P(("dom", "rep"), None),
        P(),
        P(("dom", "rep"), None, None),
        P(("dom", "rep"), None),
        P(("dom", "rep")),
        P(("dom", "rep")),
    )
    out_specs = (P(("dom", "rep"), None), P("dom", "rep"))
    return jax.shard_map(
        on_device, mesh=mesh, in_specs=in_specs, out_specs=out_specs, check_vma=False
    )
```

time: 193 us -> 125 us (0.65)
  blocking collectives: 96.2 us -> 0 us
  Pallas kernels: 21.3 us -> 114 us
  waiting for transfers between devices: 46.6 us -> 0 us
  between operations: 14.8 us -> 1.32 us
  other arithmetic: 2.44 us -> 0 us
  matrix products: 2.22 us -> 0 us
    all_to_all x3 -> x0, blocking collectives: 96.2 us -> none  [the longest x2 50.3 us: sent_and_summed(): lax.all_to_all(parts, axis, split_axis=0, concat_axis=0, tiled=True)]
    pallas_call x0 -> x2, Pallas kernels: none -> 78.2 us  [the longest x1 58.5 us: regroup(): pl.pallas_call(lambda *refs: regroup_kernel(zs_n, xs_n, ys_n, *refs), out...]
    all_gather x1 -> x0, waiting for transfers between devices: 46.6 us -> none  [on_device(): whole = lax.all_gather(local_rows, 'rep', axis=0, tiled=True)]
    pallas_call x1, Pallas kernels: 21.3 us -> 35.8 us  [slots(): pl.pallas_call(lambda *refs: slots_kernel(scale, *refs), out_shape=(jax.S...]
    unnamed x13 -> x16, local copies, waits for them, and re-layouts: 4.05 us -> 8.2 us
    another operation x2 -> x0, local copies, waits for them, and re-layouts: 3.56 us -> none  [the longest x1 2.13 us: on_device(): local_rows = arrived.reshape(row_count, feat_width)]
    dot_general x1 -> x0, matrix products: 2.22 us -> none  [on_device(): jnp.dot(onehot, grad_out, preferred_element_type=jnp.float32)]
  transfers between devices with their start and end apart: 1 -> 0, of which waited for: 1 -> 0; matrix products, arithmetic and copies ran while one was open for 0% -> 0% of each run, Pallas kernels for 0% -> 0%
where the time goes in v2:
time: 125 us; the launch traced here: 124 us
  Pallas kernels  114 us (91%)
  local copies, waits for them, and re-layouts  8.33 us (7%)
  between operations  1.32 us (1%)
    pallas_call x1, Pallas kernels, regroup(): pl.pallas_call(lambda *refs: regroup_kernel(zs_n, xs_n, ys_n, *refs), out...  58.5 us
    pallas_call x1, Pallas kernels, slots(): pl.pallas_call(lambda *refs: slots_kernel(scale, *refs), out_shape=(jax.S...  35.8 us
    pallas_call x1, Pallas kernels, reduce_parts(): pl.pallas_call(lambda *refs: reduce_kernel(zs_n, xs_n, ys_n, *refs), out_...  19.6 us
    unnamed x16, local copies, waits for them, and re-layouts  8.2 us

profile of v2, /device:TPU:1, one launch (start us, length us, event | category | flops | bytes accessed | tf_op | source)
XLA Modules:
  0.0 123.7 jit_solution(16875607102767296567)
XLA Ops:
  1.3 0.8 copy.9
  2.1 0.1 reshape.13.refs_0_
  2.2 0.0 copy-start.2
  2.2 1.2 copy-done.2
  3.4 0.0 copy-start.6
  3.4 0.7 copy-done.6
  4.1 0.0 copy-start.1
  4.1 0.0 copy-start.3
  4.1 0.0 copy-start.5
  4.1 58.5 %regroup.1 = bf16[8,8,128,512]{3,2,1,0:T(8,128)(2,1)S(1)} custom-call(s32[1,1024]{1,0:T(1,128)S(1)} %bitcast.3, bf16[1024,512]{1,0:T(8,128)(2,1)S(1)} %copy-done.2), custom_call_target="tpu_custom_call" | custom-call | tf_op jit(solution)/shard_map/regroup/pallas_call | solution.py:234
  62.7 0.0 copy-start
  62.7 3.2 %copy-done = bf16[8,8,128,512]{3,2,1,0:T(8,128)(2,1)} copy-done((bf16[8,8,128,512]{3,2,1,0:T(8,128)(2,1)}, bf16[8,8,128,512]{3,2,1,0:T(8,128)(2,1)S(1)}, u32[]{:S(2)}) %copy-start) | copy-done | bytes 8388632
  65.9 0.0 copy-done.1
  65.9 0.0 copy-done.3
  65.9 0.0 copy-done.5
  65.9 35.8 %slots.1 = (bf16[1024,512]{1,0:T(8,128)(2,1)}, f32[512,512]{1,0:T(8,128)S(1)}) custom-call(s32[256]{0:T(256)S(1)} %reshape.13.refs_0_, s32[1]{0:T(128)S(6)} %copy.11.refs_1_, bf16[64,128,512]{2,1,0:T(8,128)(2,1)} %bitcast.2, bf16[128,128,128]{2,1,0:T(8,128)(2,1)S(1)} %copy-done.1, bf16[1024,512]{1,0:T(8,128)(2,1)S(1)} %copy-done.3, ...), custom_call_target="tpu_custom_call" | custom-call | tf_op jit(solution)/shard_map/slots/pallas_call | solution.py:52
  101.8 0.0 copy-start.4
  101.8 1.0 copy-done.4
  102.7 19.6 %reduce.1 = f32[16,64]{1,0:T(8,128)} custom-call(f32[512,512]{1,0:T(8,128)} %copy-done.4), custom_call_target="tpu_custom_call" | custom-call | tf_op jit(solution)/shard_map/reduce/pallas_call | solution.py:387
  122.4 1.3 %copy.12 = f32[16,64]{1,0:T(8,128)} copy(f32[16,64]{1,0:T(8,128)} %reduce.1) | data formatting | bytes 8192
Async XLA Ops:
  2.2 1.2 copy-start.2
  3.4 0.7 copy-start.6
  4.1 61.8 %copy-start.1 = (bf16[128,128,128]{2,1,0:T(8,128)(2,1)S(1)}, bf16[128,128,128]{2,1,0:T(8,128)(2,1)}, u32[]{:S(2)}) copy-start(bf16[128,128,128]{2,1,0:T(8,128)(2,1)} %refs_3_.1) | copy-start | bytes 12582916
  4.1 61.8 %copy-start.3 = (bf16[1024,512]{1,0:T(8,128)(2,1)S(1)}, bf16[1024,512]{1,0:T(8,128)(2,1)}, u32[]{:S(2)}) copy-start(bf16[1024,512]{1,0:T(8,128)(2,1)} %refs_4_.1) | copy-start | bytes 3145732
  4.1 61.8 %copy-start.5 = (bf16[512,512]{1,0:T(8,128)(2,1)S(1)}, bf16[512,512]{1,0:T(8,128)(2,1)}, u32[]{:S(2)}) copy-start(bf16[512,512]{1,0:T(8,128)(2,1)} %refs_5_.1) | copy-start | bytes 1572868
  62.7 3.2 %copy-start = (bf16[8,8,128,512]{3,2,1,0:T(8,128)(2,1)}, bf16[8,8,128,512]{3,2,1,0:T(8,128)(2,1)S(1)}, u32[]{:S(2)}) copy-start(bf16[8,8,128,512]{3,2,1,0:T(8,128)(2,1)S(1)} %regroup.1) | copy-start | bytes 25165828
  101.8 1.0 copy-start.4

commit v3 on v2

--- a/solution.py
+++ b/solution.py
@@ -8,57 +8,99 @@
 from jax.sharding import PartitionSpec as P
 
 
-def slots_kernel(scale, index_ref, count_ref, src_ref, edge_ref, feat_ref, weight_ref,
-                 gi_ref, wg_ref, acc_ref):
-    acc_ref[...] = jnp.zeros_like(acc_ref)
-
-    @pl.loop(0, count_ref[0])
-    def _(s):
-        b = index_ref[2 * s]
-        c = index_ref[2 * s + 1]
-        acc_ref[c] += lax.dot_general(
-            edge_ref[s], src_ref[b], (((0,), (0,)), ((), ())),
+def slots_kernel(scale, depth, step, table_ref, src_ref, edge_ref, feat_ref, weight_ref,
+                 gi_ref, wg_ref, acc_ref, agg_ref, tab, tab_sem):
+    side = edge_ref.shape[1]
+    cols = agg_ref.shape[0] // side
+    copy = pltpu.make_async_copy(table_ref, tab, tab_sem)
+    copy.start()
+    copy.wait()
+
+    def product(first, count, end):
+        edges, rows = [], []
+        for g in range(count):
+            p = first + g
+            if end is not None and g > count - step:
+                q = jnp.minimum(p, end - 1)
+                e = edge_ref[tab[0, q]]
+                e = jnp.where(p < end, e, jnp.zeros_like(e))
+            else:
+                q = p
+                e = edge_ref[tab[0, q]]
+            edges.append(e)
+            rows.append(src_ref[tab[1, q]])
+        return lax.dot_general(
+            jnp.concatenate(edges, 0), jnp.concatenate(rows, 0), (((0,), (0,)), ((), ())),
             preferred_element_type=jnp.float32)
 
-    side = acc_ref.shape[1]
-
-    @pl.loop(0, acc_ref.shape[0])
+    @pl.loop(0, cols)
     def _(c):
-        rows = pl.ds(pl.multiple_of(c * side, side), side)
-        agg = acc_ref[c].astype(jnp.bfloat16)
-        gi_ref[rows, :] = lax.dot_general(
-            agg, weight_ref[...], (((1,), (1,)), ((), ())),
-            preferred_element_type=jnp.float32).astype(gi_ref.dtype)
-        part = lax.dot_general(
-            feat_ref[rows, :], agg, (((0,), (0,)), ((), ())),
-            preferred_element_type=jnp.float32)
-
-        @pl.when(c == 0)
-        def _():
-            wg_ref[...] = part
-
-        @pl.when(c > 0)
-        def _():
-            wg_ref[...] += part
-
-    wg_ref[...] = wg_ref[...] * scale
-
-
-def slots(scale, index, count, src, edge, feat, weight):
+        first = tab[2, c]
+        end = tab[2, c + 1]
+        count = end - first
+        full = jnp.maximum(count - 1, 0) // depth
+        rest = (count - full * depth + step - 1) // step
+        tail = first + full * depth
+        place = pl.ds(pl.multiple_of(c * side, side), side)
+        acc_ref[...] = jnp.zeros_like(acc_ref)
+
+        @pl.loop(0, full)
+        def _(t):
+            acc_ref[...] += product(first + t * depth, depth, None)
+
+        @pl.when(rest == 0)
+        def _():
+            agg_ref[place, :] = jnp.zeros((side, agg_ref.shape[1]), agg_ref.dtype)
+
+        for k in range(1, depth // step + 1):
+            @pl.when(rest == k)
+            def _():
+                agg_ref[place, :] = (acc_ref[...] + product(tail, k * step, end)).astype(
+                    agg_ref.dtype)
+
+    wg_ref[...] = lax.dot_general(
+        feat_ref[...], agg_ref[...], (((0,), (0,)), ((), ())),
+        preferred_element_type=jnp.float32) * scale
+    gi_ref[...] = lax.dot_general(
+        agg_ref[...], weight_ref[...], (((1,), (1,)), ((), ())),
+        preferred_element_type=jnp.float32).astype(gi_ref.dtype)
+
+
+def slots(scale, table, src, edge, feat, weight):
     rows, width = feat.shape
     side = edge.shape[1]
-    smem = pl.BlockSpec(memory_space=pltpu.SMEM)
     vmem = pl.BlockSpec(memory_space=pltpu.VMEM)
     return pl.pallas_call(
-        lambda *refs: slots_kernel(scale, *refs),
+        lambda *refs: slots_kernel(scale, 16, 4, *refs),
         out_shape=(jax.ShapeDtypeStruct((rows, weight.shape[0]), jnp.bfloat16),
                    jax.ShapeDtypeStruct((width, src.shape[2]), jnp.float32)),
-        in_specs=[smem, smem, vmem, vmem, vmem, vmem],
+        in_specs=[vmem] * 5,
         out_specs=(vmem, vmem),
-        scratch_shapes=[pltpu.VMEM((rows // side, side, src.shape[2]), jnp.float32)],
-        compiler_params=pltpu.CompilerParams(vmem_limit_bytes=40 << 20),
+        scratch_shapes=[pltpu.VMEM((side, src.shape[2]), jnp.float32),
+                        pltpu.VMEM((rows, src.shape[2]), jnp.bfloat16),
+                        pltpu.SMEM(table.shape, jnp.int32),
+                        pltpu.SemaphoreType.DMA],
+        compiler_params=pltpu.CompilerParams(vmem_limit_bytes=20 << 20),
         name="slots",
-    )(index.reshape(-1), count, src, edge, feat, weight)
+    )(table, src, edge, feat, weight)
+
+
+def slot_table(index, live):
+    count = index.shape[1]
+    here = lax.broadcasted_iota(jnp.int32, (count, count), 0)
+    lane = lax.broadcasted_iota(jnp.int32, (count, count), 1)
+    row = jnp.broadcast_to(index[0:1, :], (count, count)).astype(jnp.float32).T
+    across = jnp.where(lane < live, jnp.broadcast_to(index[1:2, :], (count, count)), count)
+    across = across.astype(jnp.float32)
+    key = across.T
+    ahead = (across < key) | ((across == key) & (lane < here))
+    rank = jnp.sum(jnp.where(ahead, 1.0, 0.0), axis=1, keepdims=True)
+    hit = rank == lane.astype(jnp.float32)
+    slot = jnp.sum(jnp.where(hit, here.astype(jnp.float32), 0.0), axis=0, keepdims=True)
+    block = jnp.sum(jnp.where(hit, row, 0.0), axis=0, keepdims=True)
+    start = jnp.sum(jnp.where(key < lane.astype(jnp.float32), 1.0, 0.0), axis=0, keepdims=True)
+    rest = jnp.zeros((5, count), jnp.float32)
+    return jnp.concatenate([slot, block, start, rest], axis=0).astype(jnp.int32)
 
 
 MESH = pl.DeviceIdType.MESH
@@ -68,7 +110,8 @@
     return lax.rem(value + 2 * size, size)
 
 
-def regroup_kernel(zs_n, xs_n, ys_n, perm_ref, grad_ref, out_ref, ordered, raw, unperm,
+def regroup_kernel(zs_n, xs_n, ys_n, perm_hbm, grad_hbm, index_hbm, count_ref, out_ref,
+                   table_ref, grad_ref, perm_ref, index_ref, load_sem, ordered, raw, unperm,
                    own_sem, a_send, a_recv, y_send, y_recv, f_send, f_recv, p_send, p_recv):
     d = lax.axis_index("dom")
     r = lax.axis_index("rep")
@@ -86,6 +129,12 @@
         return ((j + 1) // 2) * (2 * lax.rem(j, 2) - 1)
 
     barrier = pltpu.get_barrier_semaphore()
+    grad_load = pltpu.make_async_copy(grad_hbm, grad_ref, load_sem.at[0])
+    grad_load.start()
+    perm_load = pltpu.make_async_copy(perm_hbm, perm_ref, load_sem.at[1])
+    perm_load.start()
+    index_load = pltpu.make_async_copy(index_hbm, index_ref, load_sem.at[2])
+    index_load.start()
 
     @pl.loop(1, peers)
     def _(n):
@@ -96,9 +145,11 @@
         pl.semaphore_signal(barrier, inc=1, device_id={"dom": d, "rep": other},
                             device_id_type=MESH)
 
+    perm_load.wait()
     perm = perm_ref[...]
     target = (perm // grad_ref.shape[0]) * slot_rows + lax.rem(perm, slot_rows)
     tile = 256
+    grad_load.wait()
 
     @pl.loop(0, grad_ref.shape[0] // tile)
     def _(t):
@@ -108,29 +159,31 @@
             hot, grad_ref[...], (((1,), (0,)), ((), ())),
             preferred_element_type=jnp.float32).astype(jnp.bfloat16)
 
+    pl.semaphore_wait(barrier, peers - 1 + 3)
+
+    own = pltpu.make_async_copy(
+        ordered.at[pl.ds(pl.multiple_of(d * piece, piece), piece)], raw.at[z, x, r], own_sem)
+    own.start()
+
+    def a_copy(n, zs, xs):
+        j, i = n // xs_n, lax.rem(n, xs_n)
+        to = wrap(z + offset(j), zs_n) * xs_n + wrap(x + i, xs_n)
+        return pltpu.make_async_remote_copy(
+            src_ref=ordered.at[pl.ds(pl.multiple_of(to * piece, piece), piece)],
+            dst_ref=raw.at[zs, xs, r],
+            send_sem=a_send.at[n], recv_sem=a_recv.at[n],
+            device_id={"dom": to, "rep": r}, device_id_type=MESH)
+
+    @pl.loop(1, peers)
+    def _(n):
+        a_copy(n, z, x).start()
+
+    index_load.wait()
+    table_ref[...] = slot_table(index_ref[...], count_ref[0])
     q = lax.broadcasted_iota(jnp.int32, (tile, tile), 0)
     p = lax.broadcasted_iota(jnp.int32, (tile, tile), 1)
     wanted = lax.rem(q // slot_rows, 8) * piece + (q // piece) * slot_rows + lax.rem(q, slot_rows)
     unperm[...] = jnp.where(p == wanted, 1.0, 0.0).astype(jnp.bfloat16)
-
-    pl.semaphore_wait(barrier, peers - 1 + 3)
-
-    own = pltpu.make_async_copy(
-        ordered.at[pl.ds(pl.multiple_of(d * piece, piece), piece)], raw.at[z, x, r], own_sem)
-    own.start()
-
-    def a_copy(n, zs, xs):
-        j, i = n // xs_n, lax.rem(n, xs_n)
-        to = wrap(z + offset(j), zs_n) * xs_n + wrap(x + i, xs_n)
-        return pltpu.make_async_remote_copy(
-            src_ref=ordered.at[pl.ds(pl.multiple_of(to * piece, piece), piece)],
-            dst_ref=raw.at[zs, xs, r],
-            send_sem=a_send.at[n], recv_sem=a_recv.at[n],
-            device_id={"dom": to, "rep": r}, device_id_type=MESH)
-
-    @pl.loop(1, peers)
-    def _(n):
-        a_copy(n, z, x).start()
 
     def chunk_of(j):
         return wrap(z - offset(j), zs_n)
@@ -224,19 +277,24 @@
             p_copy(j, which, r).wait_send()
 
 
-def regroup(perm, grad, sizes):
+def regroup(perm, grad, index, count, sizes):
     zs_n, xs_n, ys_n = sizes
     rows, width = grad.shape
     reps, doms = 2 * ys_n, zs_n * xs_n
     piece = rows // doms
     vmem = pl.BlockSpec(memory_space=pltpu.VMEM)
     dma = pltpu.SemaphoreType.DMA
+    far = pl.BlockSpec(memory_space=pltpu.HBM)
     return pl.pallas_call(
         lambda *refs: regroup_kernel(zs_n, xs_n, ys_n, *refs),
-        out_shape=jax.ShapeDtypeStruct((reps, zs_n, rows // zs_n, width), grad.dtype),
-        in_specs=[vmem, vmem],
-        out_specs=vmem,
+        out_shape=(jax.ShapeDtypeStruct((reps, zs_n, rows // zs_n, width), grad.dtype),
+                   jax.ShapeDtypeStruct((8, index.shape[1]), jnp.int32)),
+        in_specs=[far, far, far, pl.BlockSpec(memory_space=pltpu.SMEM)],
+        out_specs=(vmem, vmem),
+        cost_estimate=pl.CostEstimate(flops=40*10**9, bytes_accessed=150*10**6, transcendentals=0),
         scratch_shapes=[
+            pltpu.VMEM((rows, width), grad.dtype), pltpu.VMEM((1, rows), jnp.int32),
+            pltpu.VMEM(index.shape, jnp.int32), dma((3,)),
             pltpu.VMEM((rows, width), grad.dtype),
             pltpu.VMEM((zs_n, xs_n, reps, piece, width), grad.dtype),
             pltpu.VMEM((256, 256), grad.dtype),
@@ -245,9 +303,9 @@
             dma((4, zs_n)), dma((4, zs_n)),
         ],
         compiler_params=pltpu.CompilerParams(
-            collective_id=0, has_side_effects=True, vmem_limit_bytes=32 << 20),
+            collective_id=0, has_side_effects=True, vmem_limit_bytes=14 << 20),
         name="regroup",
-    )(perm.reshape(1, rows), grad)
+    )(perm.reshape(1, rows), grad, index, count)
 
 
 def reduce_kernel(zs_n, xs_n, ys_n, part_ref, out_ref, pair_in, y_in, half_sum, cols_sum, dom_in,
@@ -396,7 +454,8 @@
             dma((ys_n,)), dma((ys_n,)), dma((ys_n,)), dma((ys_n,)),
             dma((doms // 2,)), dma((doms,)), dma, dma,
         ],
-        compiler_params=pltpu.CompilerParams(collective_id=1, has_side_effects=True),
+        compiler_params=pltpu.CompilerParams(
+            collective_id=1, has_side_effects=True, vmem_limit_bytes=8 << 20),
         name="reduce",
     )(part)
 
@@ -406,10 +465,11 @@
 
 def on_device(grad_out, features, weight, edge_blocks, block_index, block_count, node_perm):
     block_side = edge_blocks.shape[1]
-    stacked = regroup(node_perm, grad_out, SIZES).reshape(-1, block_side, grad_out.shape[1])
+    stacked, table = regroup(node_perm, grad_out, block_index.T, block_count, SIZES)
+    stacked = stacked.reshape(-1, block_side, grad_out.shape[1])
     nodes = grad_out.shape[0] * lax.axis_size("dom") * lax.axis_size("rep")
     grad_input, partial = slots(
-        1.0 / math.sqrt(nodes), block_index, block_count, stacked, edge_blocks, features, weight)
+        1.0 / math.sqrt(nodes), table, stacked, edge_blocks, features, weight)
     return (grad_input, reduce_parts(partial, SIZES))
 
 

time: 125 us -> 92 us (0.74)
  Pallas kernels: 114 us -> 86.9 us
  local copies, waits for them, and re-layouts: 8.33 us -> 3.19 us
    pallas_call x1, Pallas kernels: 35.8 us -> 5.9 us  [slots(): pl.pallas_call(lambda *refs: slots_kernel(scale, 16, 4, *refs), out_shape...]
    unnamed x16 -> x13, local copies, waits for them, and re-layouts: 8.2 us -> 3.19 us
    pallas_call x1, Pallas kernels: 19.6 us -> 22.3 us  [reduce_parts(): pl.pallas_call(lambda *refs: reduce_kernel(zs_n, xs_n, ys_n, *refs), out_...]
where the time goes in v3:
time: 92 us; the launch traced here: 91.4 us
  Pallas kernels  86.9 us (94%)
  local copies, waits for them, and re-layouts  3.19 us (3%)
  between operations  1.34 us (1%)
    pallas_call x1, Pallas kernels, regroup(): pl.pallas_call(lambda *refs: regroup_kernel(zs_n, xs_n, ys_n, *refs), out...  58.7 us
    pallas_call x1, Pallas kernels, reduce_parts(): pl.pallas_call(lambda *refs: reduce_kernel(zs_n, xs_n, ys_n, *refs), out_...  22.3 us
    pallas_call x1, Pallas kernels, slots(): pl.pallas_call(lambda *refs: slots_kernel(scale, 16, 4, *refs), out_shape...  5.9 us
    unnamed x13, local copies, waits for them, and re-layouts  3.19 us

profile of v3, /device:TPU:1, one launch (start us, length us, event | category | flops | bytes accessed | tf_op | source)
XLA Modules:
  0.0 91.4 jit_solution(9740130407942355036)
XLA Ops:
  1.3 0.0 copy-start.3
  1.3 1.2 %copy-done.3 = bf16[1024,512]{1,0:T(8,128)(2,1)S(1)} copy-done((bf16[1024,512]{1,0:T(8,128)(2,1)S(1)}, bf16[1024,512]{1,0:T(8,128)(2,1)}, u32[]{:S(2)}) %copy-start.3) | copy-done | bytes 1048600
  2.5 0.0 copy-start.4
  2.5 0.7 copy-done.4
  3.2 0.0 copy-start.5
  3.2 0.7 copy-done.5
  3.9 0.0 copy-start
  3.9 0.0 copy-start.1
  3.9 0.0 copy-start.2
  3.9 58.7 %regroup.1 = (bf16[8,8,128,512]{3,2,1,0:T(8,128)(2,1)S(1)}, s32[8,128]{1,0:T(8,128)S(1)}) custom-call(s32[1,1024]{1,0:T(1,128)S(1)} %bitcast.4, bf16[1024,512]{1,0:T(8,128)(2,1)S(1)} %copy-done.3, s32[2,128]{1,0:T(2,128)S(1)} %bitcast.5, s32[1]{0:T(128)S(6)} %copy.10.refs_3_), custom_call_target="tpu_custom_call" | custom-call | flops 40000000000 | bytes 150000000 | tf_op jit(solution)/shard_map/regroup/pallas_call | solution.py:288
  62.6 0.0 copy-done
  62.6 0.0 copy-done.1
  62.6 0.0 copy-done.2
  62.6 5.9 %slots.1 = (bf16[1024,512]{1,0:T(8,128)(2,1)}, f32[512,512]{1,0:T(8,128)S(1)}) custom-call(s32[8,128]{1,0:T(8,128)S(1)} %get-tuple-element.6.refs_0_, bf16[64,128,512]{2,1,0:T(8,128)(2,1)S(1)} %bitcast.3, bf16[128,128,128]{2,1,0:T(8,128)(2,1)S(1)} %copy-done, bf16[1024,512]{1,0:T(8,128)(2,1)S(1)} %copy-done.1, bf16[512,512]{1,0:T(8,128)(2,1)S(1)} %copy-done.2), custom_call_target="tpu_custom_call" | custom-call | tf_op jit(solution)/shard_map/slots/pallas_call | solution.py:73
  68.6 22.3 %reduce.1 = f32[16,64]{1,0:T(8,128)S(1)} custom-call(f32[512,512]{1,0:T(8,128)S(1)} %get-tuple-element.9.refs_0_), custom_call_target="tpu_custom_call" | custom-call | tf_op jit(solution)/shard_map/reduce/pallas_call | solution.py:445
  90.8 0.6 copy.11
Async XLA Ops:
  1.3 1.2 %copy-start.3 = (bf16[1024,512]{1,0:T(8,128)(2,1)S(1)}, bf16[1024,512]{1,0:T(8,128)(2,1)}, u32[]{:S(2)}) copy-start(bf16[1024,512]{1,0:T(8,128)(2,1)} %refs_1_.1) | copy-start | bytes 3145732
  2.5 0.7 copy-start.4
  3.2 0.7 copy-start.5
  3.9 58.7 %copy-start = (bf16[128,128,128]{2,1,0:T(8,128)(2,1)S(1)}, bf16[128,128,128]{2,1,0:T(8,128)(2,1)}, u32[]{:S(2)}) copy-start(bf16[128,128,128]{2,1,0:T(8,128)(2,1)} %refs_2_.1) | copy-start | bytes 12582916
  3.9 58.8 %copy-start.1 = (bf16[1024,512]{1,0:T(8,128)(2,1)S(1)}, bf16[1024,512]{1,0:T(8,128)(2,1)}, u32[]{:S(2)}) copy-start(bf16[1024,512]{1,0:T(8,128)(2,1)} %refs_3_.2) | copy-start | bytes 3145732
  3.9 58.8 %copy-start.2 = (bf16[512,512]{1,0:T(8,128)(2,1)S(1)}, bf16[512,512]{1,0:T(8,128)(2,1)}, u32[]{:S(2)}) copy-start(bf16[512,512]{1,0:T(8,128)(2,1)} %refs_4_.1) | copy-start | bytes 1572868

commit v4 on v3

--- a/solution.py
+++ b/solution.py
@@ -8,8 +8,8 @@
 from jax.sharding import PartitionSpec as P
 
 
-def slots_kernel(scale, depth, step, table_ref, src_ref, edge_ref, feat_ref, weight_ref,
-                 gi_ref, wg_ref, acc_ref, agg_ref, tab, tab_sem):
+def slots_kernel(depth, step, table_ref, src_ref, edge_ref, weight_ref,
+                 gi_ref, agg_ref, acc_ref, tab, tab_sem):
     side = edge_ref.shape[1]
     cols = agg_ref.shape[0] // side
     copy = pltpu.make_async_copy(table_ref, tab, tab_sem)
@@ -58,31 +58,27 @@
                 agg_ref[place, :] = (acc_ref[...] + product(tail, k * step, end)).astype(
                     agg_ref.dtype)
 
-    wg_ref[...] = lax.dot_general(
-        feat_ref[...], agg_ref[...], (((0,), (0,)), ((), ())),
-        preferred_element_type=jnp.float32) * scale
     gi_ref[...] = lax.dot_general(
         agg_ref[...], weight_ref[...], (((1,), (1,)), ((), ())),
         preferred_element_type=jnp.float32).astype(gi_ref.dtype)
 
 
-def slots(scale, table, src, edge, feat, weight):
-    rows, width = feat.shape
+def slots(table, src, edge, weight):
     side = edge.shape[1]
+    rows = src.shape[0] * side // 8
     vmem = pl.BlockSpec(memory_space=pltpu.VMEM)
     return pl.pallas_call(
-        lambda *refs: slots_kernel(scale, 16, 4, *refs),
+        lambda *refs: slots_kernel(16, 4, *refs),
         out_shape=(jax.ShapeDtypeStruct((rows, weight.shape[0]), jnp.bfloat16),
-                   jax.ShapeDtypeStruct((width, src.shape[2]), jnp.float32)),
-        in_specs=[vmem] * 5,
+                   jax.ShapeDtypeStruct((rows, src.shape[2]), jnp.bfloat16)),
+        in_specs=[vmem] * 4,
         out_specs=(vmem, vmem),
         scratch_shapes=[pltpu.VMEM((side, src.shape[2]), jnp.float32),
-                        pltpu.VMEM((rows, src.shape[2]), jnp.bfloat16),
                         pltpu.SMEM(table.shape, jnp.int32),
                         pltpu.SemaphoreType.DMA],
         compiler_params=pltpu.CompilerParams(vmem_limit_bytes=20 << 20),
         name="slots",
-    )(table, src, edge, feat, weight)
+    )(table, src, edge, weight)
 
 
 def slot_table(index, live):
@@ -308,156 +304,184 @@
     )(perm.reshape(1, rows), grad, index, count)
 
 
-def reduce_kernel(zs_n, xs_n, ys_n, part_ref, out_ref, pair_in, y_in, half_sum, cols_sum, dom_in,
-                  result, c_send, c_recv, y_send, y_recv, d_send, d_recv, l_send, l_recv):
+def reduce_kernel(zs_n, xs_n, ys_n, scale, stage, agg_ref, feat_ref, out_ref, part_other, part_mine,
+                  pair_in, sums, far_in, y_in, cols_sum, packed, dom_in,
+                  c_send, c_recv, s_send, s_recv, y_send, y_recv, d_send, d_recv):
     d = lax.axis_index("dom")
     r = lax.axis_index("rep")
     y, c = r // 2, lax.rem(r, 2)
     doms = zs_n * xs_n
     group = doms // 2
     rows = out_ref.shape[0]
-    lanes = 2 * out_ref.shape[1]
-    tall = group * rows
+    tall, lanes = cols_sum.shape
+    mid = tall // 2
     r_pair = r + 1 - 2 * c
-    takes = d // group == c
+    r_way = (wrap(y + 1, ys_n) * 2 + c, wrap(y - 1, ys_n) * 2 + c)
+    home = d // group
     barrier = pltpu.get_barrier_semaphore()
 
-    @pl.when(takes)
+    for other in (*r_way, r_pair):
+        pl.semaphore_signal(barrier, inc=1, device_id={"dom": d, "rep": other},
+                            device_id_type=MESH)
+
+    @pl.loop(0, doms)
+    def _(n):
+        @pl.when((n > 0) | (c != home))
+        def _():
+            pl.semaphore_signal(barrier, inc=1,
+                                device_id={"dom": wrap(d + n, doms), "rep": y * 2 + home},
+                                device_id_type=MESH)
+
+    def partial(half):
+        cols = feat_ref[:, pl.ds(pl.multiple_of(half * tall, tall), tall)]
+        return lax.dot_general(
+            cols, agg_ref[...], (((0,), (0,)), ((), ())),
+            preferred_element_type=jnp.float32) * scale
+
+    part_other[...] = partial(1 - c)
+
+    @pl.when(c == home)
     def _():
-        @pl.loop(1, doms)
-        def _(n):
-            pl.semaphore_signal(barrier, inc=1, device_id={"dom": wrap(d + n, doms), "rep": r},
-                                device_id_type=MESH)
-
-    @pl.loop(1, ys_n)
-    def _(n):
-        pl.semaphore_signal(barrier, inc=1,
-                            device_id={"dom": d, "rep": wrap(y + n, ys_n) * 2 + c},
-                            device_id_type=MESH)
-
-    pl.semaphore_signal(barrier, inc=1, device_id={"dom": d, "rep": r_pair}, device_id_type=MESH)
-
-    @pl.when(takes)
+        pl.semaphore_wait(barrier, doms - 1 + 3)
+
+    @pl.when(c != home)
     def _():
-        pl.semaphore_wait(barrier, group - 1 + ys_n)
-
-    @pl.when(jnp.logical_not(takes))
-    def _():
-        pl.semaphore_wait(barrier, group + ys_n)
+        pl.semaphore_wait(barrier, doms + 3)
 
     def wide(n):
         return pl.ds(pl.multiple_of(wrap(y + n, ys_n) * lanes, lanes), lanes)
 
-    order = (2, 1, 3, 0)
-    mine = pl.ds(pl.multiple_of(c * tall, tall), tall)
-    other = pl.ds(pl.multiple_of((1 - c) * tall, tall), tall)
-
     def c_copy(n):
         return pltpu.make_async_remote_copy(
-            src_ref=part_ref.at[other, wide(n)], dst_ref=pair_in.at[n],
+            src_ref=part_other.at[:, wide(n)], dst_ref=pair_in.at[n],
             send_sem=c_send.at[n], recv_sem=c_recv.at[n],
             device_id={"dom": d, "rep": r_pair}, device_id_type=MESH)
 
-    def y_copy(n):
-        return pltpu.make_async_remote_copy(
-            src_ref=half_sum.at[n], dst_ref=y_in.at[n],
-            send_sem=y_send.at[n], recv_sem=y_recv.at[n],
-            device_id={"dom": d, "rep": wrap(y + n, ys_n) * 2 + c}, device_id_type=MESH)
-
-    for n in order:
-        c_copy(n).start()
-    for n in order:
+    def s_copy(way):
+        return pltpu.make_async_remote_copy(
+            src_ref=sums.at[2, pl.ds(way * mid, mid)], dst_ref=far_in.at[way],
+            send_sem=s_send.at[way], recv_sem=s_recv.at[way],
+            device_id={"dom": d, "rep": r_way[way]}, device_id_type=MESH)
+
+    def y_copy(way, part):
+        place = pl.ds(part * mid, mid)
+        return pltpu.make_async_remote_copy(
+            src_ref=sums.at[1 + 2 * way, place], dst_ref=y_in.at[way, place],
+            send_sem=y_send.at[way, part], recv_sem=y_recv.at[way, part],
+            device_id={"dom": d, "rep": r_way[way]}, device_id_type=MESH)
+
+    def add_pair(n):
         c_copy(n).wait_recv()
-        half_sum[n] = part_ref[mine, wide(n)] + pair_in[n]
-        if n:
-            y_copy(n).start()
-    for n in (1, 3, 2):
-        y_copy(n).wait_recv()
-    cols_sum[...] = (half_sum[0] + y_in[1]) + (y_in[2] + y_in[3])
-
-    def d_copy(n):
-        return pltpu.make_async_remote_copy(
-            src_ref=cols_sum.at[pl.ds(pl.multiple_of(n * rows, rows), rows)],
-            dst_ref=dom_in.at[d],
-            send_sem=d_send.at[n], recv_sem=d_recv.at[d],
-            device_id={"dom": c * group + n, "rep": r}, device_id_type=MESH)
-
-    @pl.loop(0, group)
-    def _(m):
-        n = lax.rem(m + d, group)
-
-        @pl.when(c * group + n != d)
-        def _():
-            d_copy(n).start()
-
-    def l_copy():
-        return pltpu.make_async_remote_copy(
-            src_ref=result, dst_ref=result, send_sem=l_send, recv_sem=l_recv,
-            device_id={"dom": d, "rep": r_pair}, device_id_type=MESH)
-
-    @pl.when(takes)
-    def _():
-        dom_in[d] = cols_sum[pl.ds(pl.multiple_of((d - c * group) * rows, rows), rows), :]
+        sums[n] = part_mine[:, wide(n)] + pair_in[n]
+
+    if stage >= 1:
+        for n in (2, 1, 3, 0):
+            c_copy(n).start()
+        part_mine[...] = partial(c)
+        add_pair(2)
+        if stage >= 2:
+            for way in range(2):
+                s_copy(way).start()
+        for way in range(2):
+            add_pair(1 + 2 * way)
+            if stage >= 2:
+                y_copy(way, 1 - way).start()
+        add_pair(0)
+    if stage >= 2:
+        for way in range(2):
+            s_copy(way).wait_recv()
+            sums[1 + 2 * way, way * mid:(way + 1) * mid] += far_in[way]
+            y_copy(way, way).start()
+        for way in range(2):
+            y_copy(way, 1 - way).wait_recv()
+        for way in range(2):
+            y_copy(way, way).wait_recv()
+        cols_sum[...] = sums[0] + (y_in[0] + y_in[1])
+    both = cols_sum[...].reshape(group, rows, lanes)
+    low, high = both[:, :rows // 2], both[:, rows // 2:]
+    left = lax.broadcasted_iota(jnp.int32, low.shape, 2) < lanes // 2
+    packed[0] = jnp.where(left, low, pltpu.roll(high, lanes // 2, 2))
+    packed[1] = jnp.where(left, pltpu.roll(low, lanes // 2, 2), high)
+
+    def d_copy(n, core):
+        return pltpu.make_async_remote_copy(
+            src_ref=packed.at[core, n], dst_ref=dom_in.at[d],
+            send_sem=d_send.at[core, n], recv_sem=d_recv.at[d],
+            device_id={"dom": c * group + n, "rep": y * 2 + core}, device_id_type=MESH)
+
+    if stage >= 3:
+        @pl.loop(0, group)
+        def _(m):
+            n = lax.rem(m + d + group // 2, group)
+            for core in range(2):
+                @pl.when((c * group + n != d) | (c != core))
+                def _():
+                    d_copy(n, core).start()
+
+        @pl.when(c == home)
+        def _():
+            dom_in[d] = packed[c, d - c * group]
 
         @pl.loop(0, doms)
         def _(s):
-            @pl.when(s != d)
+            @pl.when((s != d) | (c != home))
             def _():
                 pltpu.make_async_remote_copy(
-                    src_ref=cols_sum.at[pl.ds(0, rows)], dst_ref=dom_in.at[s],
-                    send_sem=d_send.at[0], recv_sem=d_recv.at[s],
+                    src_ref=packed.at[0, 0], dst_ref=dom_in.at[s],
+                    send_sem=d_send.at[0, 0], recv_sem=d_recv.at[s],
                     device_id={"dom": d, "rep": r_pair}, device_id_type=MESH).wait_recv()
 
-        total = dom_in[0]
-        for s in range(1, doms):
-            total = total + dom_in[s]
-        result[...] = total
-        l_copy().start()
-        l_copy().wait_send()
-
-    @pl.when(jnp.logical_not(takes))
-    def _():
-        l_copy().wait_recv()
-
-    got = result[...]
-    out_ref[...] = jnp.where(c == 0, got[:, : lanes // 2], got[:, lanes // 2 :])
-
-    for n in order:
-        c_copy(n).wait_send()
-        if n:
-            y_copy(n).wait_send()
-
-    @pl.loop(0, group)
-    def _(n):
-        @pl.when(c * group + n != d)
-        def _():
-            d_copy(n).wait_send()
-
-
-def reduce_parts(part, sizes):
+    sums_of = [dom_in[s] for s in range(doms)]
+    while len(sums_of) > 1:
+        sums_of = [a + b for a, b in zip(sums_of[::2], sums_of[1::2])]
+    total = sums_of[0]
+    out_ref[:rows // 2] = total[:, :lanes // 2]
+    out_ref[rows // 2:] = total[:, lanes // 2:]
+
+    if stage >= 1:
+        for n in range(ys_n):
+            c_copy(n).wait_send()
+    if stage >= 2:
+        for way in range(2):
+            s_copy(way).wait_send()
+            for part in range(2):
+                y_copy(way, part).wait_send()
+    if stage >= 3:
+        @pl.loop(0, group)
+        def _(n):
+            for core in range(2):
+                @pl.when((c * group + n != d) | (c != core))
+                def _():
+                    d_copy(n, core).wait_send()
+
+
+def reduce_parts(scale, agg, feat, sizes, stage=3):
     zs_n, xs_n, ys_n = sizes
-    rows, cols = part.shape
+    rows, cols = feat.shape[1], agg.shape[1]
     doms = zs_n * xs_n
     tall, lanes = rows // 2, cols // ys_n
     vmem = pl.BlockSpec(memory_space=pltpu.VMEM)
     dma = pltpu.SemaphoreType.DMA
     f32 = jnp.float32
     return pl.pallas_call(
-        lambda *refs: reduce_kernel(zs_n, xs_n, ys_n, *refs),
+        lambda *refs: reduce_kernel(zs_n, xs_n, ys_n, scale, stage, *refs),
         out_shape=jax.ShapeDtypeStruct((rows // doms, lanes // 2), f32),
-        in_specs=[vmem],
+        in_specs=[vmem, vmem],
         out_specs=vmem,
         scratch_shapes=[
+            pltpu.VMEM((tall, cols), f32), pltpu.VMEM((tall, cols), f32),
             pltpu.VMEM((ys_n, tall, lanes), f32), pltpu.VMEM((ys_n, tall, lanes), f32),
-            pltpu.VMEM((ys_n, tall, lanes), f32), pltpu.VMEM((tall, lanes), f32),
-            pltpu.VMEM((doms, rows // doms, lanes), f32), pltpu.VMEM((rows // doms, lanes), f32),
-            dma((ys_n,)), dma((ys_n,)), dma((ys_n,)), dma((ys_n,)),
-            dma((doms // 2,)), dma((doms,)), dma, dma,
+            pltpu.VMEM((2, tall // 2, lanes), f32), pltpu.VMEM((2, tall, lanes), f32),
+            pltpu.VMEM((tall, lanes), f32),
+            pltpu.VMEM((2, doms // 2, rows // doms // 2, lanes), f32),
+            pltpu.VMEM((doms, rows // doms // 2, lanes), f32),
+            dma((ys_n,)), dma((ys_n,)), dma((2,)), dma((2,)), dma((2, 2)), dma((2, 2)),
+            dma((2, doms // 2)), dma((doms,)),
         ],
         compiler_params=pltpu.CompilerParams(
-            collective_id=1, has_side_effects=True, vmem_limit_bytes=8 << 20),
+            collective_id=1, has_side_effects=True, vmem_limit_bytes=12 << 20),
         name="reduce",
-    )(part)
+    )(agg, feat)
 
 
 SIZES = (8, 4, 4)
@@ -468,9 +492,8 @@
     stacked, table = regroup(node_perm, grad_out, block_index.T, block_count, SIZES)
     stacked = stacked.reshape(-1, block_side, grad_out.shape[1])
     nodes = grad_out.shape[0] * lax.axis_size("dom") * lax.axis_size("rep")
-    grad_input, partial = slots(
-        1.0 / math.sqrt(nodes), table, stacked, edge_blocks, features, weight)
-    return (grad_input, reduce_parts(partial, SIZES))
+    grad_input, aggregated = slots(table, stacked, edge_blocks, weight)
+    return (grad_input, reduce_parts(1.0 / math.sqrt(nodes), aggregated, features, SIZES))
 
 
 def solution(mesh):

time: 92 us -> 92.3 us (level)
  no operation moved by 1% of the time
where the time goes in v4:
time: 92.3 us; the launch traced here: 91.9 us
  Pallas kernels  87.3 us (95%)
  local copies, waits for them, and re-layouts  3.2 us (3%)
  between operations  1.34 us (1%)
    pallas_call x1, Pallas kernels, regroup(): pl.pallas_call(lambda *refs: regroup_kernel(zs_n, xs_n, ys_n, *refs), out...  58.7 us
    pallas_call x1, Pallas kernels, reduce_parts(): pl.pallas_call(lambda *refs: reduce_kernel(zs_n, xs_n, ys_n, scale, stage...  23.9 us
    pallas_call x1, Pallas kernels, slots(): pl.pallas_call(lambda *refs: slots_kernel(16, 4, *refs), out_shape=(jax.S...  4.74 us
    unnamed x13, local copies, waits for them, and re-layouts  3.2 us

profile of v4, /device:TPU:1, one launch (start us, length us, event | category | flops | bytes accessed | tf_op | source)
XLA Modules:
  0.0 91.9 jit_solution(3900304617548432803)
XLA Ops:
  1.3 0.0 copy-start.3
  1.3 1.2 %copy-done.3 = bf16[1024,512]{1,0:T(8,128)(2,1)S(1)} copy-done((bf16[1024,512]{1,0:T(8,128)(2,1)S(1)}, bf16[1024,512]{1,0:T(8,128)(2,1)}, u32[]{:S(2)}) %copy-start.3) | copy-done | bytes 1048600
  2.5 0.0 copy-start.4
  2.5 0.7 copy-done.4
  3.2 0.0 copy-start.5
  3.2 0.7 copy-done.5
  3.9 0.0 copy-start
  3.9 0.0 copy-start.2
  3.9 58.7 %regroup.1 = (bf16[8,8,128,512]{3,2,1,0:T(8,128)(2,1)S(1)}, s32[8,128]{1,0:T(8,128)S(1)}) custom-call(s32[1,1024]{1,0:T(1,128)S(1)} %bitcast.4, bf16[1024,512]{1,0:T(8,128)(2,1)S(1)} %copy-done.3, s32[2,128]{1,0:T(2,128)S(1)} %bitcast.5, s32[1]{0:T(128)S(6)} %copy.10.refs_3_), custom_call_target="tpu_custom_call" | custom-call | flops 40000000000 | bytes 150000000 | tf_op jit(solution)/shard_map/regroup/pallas_call | solution.py:284
  62.6 0.0 copy-start.1
  62.6 0.0 copy-done
  62.6 0.0 copy-done.2
  62.6 4.7 %slots.1 = (bf16[1024,512]{1,0:T(8,128)(2,1)}, bf16[1024,512]{1,0:T(8,128)(2,1)S(1)}) custom-call(s32[8,128]{1,0:T(8,128)S(1)} %get-tuple-element.6.refs_0_, bf16[64,128,512]{2,1,0:T(8,128)(2,1)S(1)} %bitcast.3, bf16[128,128,128]{2,1,0:T(8,128)(2,1)S(1)} %copy-done, bf16[512,512]{1,0:T(8,128)(2,1)S(1)} %copy-done.2), custom_call_target="tpu_custom_call" | custom-call | tf_op jit(solution)/shard_map/slots/pallas_call | solution.py:70
  67.4 0.0 copy-done.1
  67.4 23.9 %reduce.1 = f32[16,64]{1,0:T(8,128)S(1)} custom-call(bf16[1024,512]{1,0:T(8,128)(2,1)S(1)} %get-tuple-element.9.refs_0_, bf16[1024,512]{1,0:T(8,128)(2,1)S(1)} %copy-done.1), custom_call_target="tpu_custom_call" | custom-call | tf_op jit(solution)/shard_map/reduce/pallas_call | solution.py:466
  91.3 0.6 copy.11
Async XLA Ops:
  1.3 1.2 %copy-start.3 = (bf16[1024,512]{1,0:T(8,128)(2,1)S(1)}, bf16[1024,512]{1,0:T(8,128)(2,1)}, u32[]{:S(2)}) copy-start(bf16[1024,512]{1,0:T(8,128)(2,1)} %refs_1_.2) | copy-start | bytes 3145732
  2.5 0.7 copy-start.4
  3.2 0.7 copy-start.5
  3.9 58.8 %copy-start = (bf16[128,128,128]{2,1,0:T(8,128)(2,1)S(1)}, bf16[128,128,128]{2,1,0:T(8,128)(2,1)}, u32[]{:S(2)}) copy-start(bf16[128,128,128]{2,1,0:T(8,128)(2,1)} %refs_2_.1) | copy-start | bytes 12582916
  3.9 58.8 %copy-start.2 = (bf16[512,512]{1,0:T(8,128)(2,1)S(1)}, bf16[512,512]{1,0:T(8,128)(2,1)}, u32[]{:S(2)}) copy-start(bf16[512,512]{1,0:T(8,128)(2,1)} %refs_3_.2) | copy-start | bytes 1572868
  62.6 4.8 %copy-start.1 = (bf16[1024,512]{1,0:T(8,128)(2,1)S(1)}, bf16[1024,512]{1,0:T(8,128)(2,1)}, u32[]{:S(2)}) copy-start(bf16[1024,512]{1,0:T(8,128)(2,1)} %refs_1_.3) | copy-start | bytes 3145732

commit v5 on v2

v5 whole, which is shorter than its diff:
```python
import math

import jax
import jax.numpy as jnp
from jax import lax
from jax.experimental import pallas as pl
from jax.experimental.pallas import tpu as pltpu
from jax.sharding import PartitionSpec as P

MESH = pl.DeviceIdType.MESH
SIZES = (8, 4, 4)


def wrap(value, size):
    return lax.rem(value + 2 * size, size)


def make_table(index, live):
    count = index.shape[1]
    here = lax.broadcasted_iota(jnp.int32, (count, count), 0).astype(jnp.float32)
    lane = lax.broadcasted_iota(jnp.int32, (count, count), 1)
    pair = jnp.broadcast_to(index[0:1, :] * 8 + index[1:2, :], (count, count))
    across = jnp.where(lane < live, pair, 4 * count).astype(jnp.float32)
    lane = lane.astype(jnp.float32)
    key = across.T

    def total(mask, value=1.0):
        return jnp.sum(jnp.where(mask, value, 0.0), axis=0, keepdims=True)

    ahead = (across < key) | ((across == key) & (lane < here))
    rank = jnp.sum(jnp.where(ahead, 1.0, 0.0), axis=1, keepdims=True)
    slot = total(rank == lane, here)
    now = total(rank == lane, key)
    before = total(rank == lane - 1.0, key)
    same = jnp.where((now == before) & (lane[0:1] > 0.0), 1.0, 0.0)
    rows = [slot, same]
    for part in range(4):
        wanted = lane + float(part * count)
        found = total(key <= wanted) - 1.0
        rows.append(jnp.where(total(key == wanted) > 0.0, found, float(count)))
    rows.append(jnp.zeros((2, count), jnp.float32))
    return jnp.concatenate(rows, axis=0).astype(jnp.int32)


def layer_kernel(
        zs_n, xs_n, ys_n, scale,
        perm_hbm, grad_hbm, index_hbm, count_ref, edge_hbm, feat_hbm, weight_hbm,
        gi_ref, out_ref,
        perm_ref, grad_ref, index_ref, edge_ref, feat_ref, weight_ref, ordered, raw, unperm,
        table_ref, tab, running, summed, dense, chunk, acc, agg_ref,
        part_other, part_mine, pair_in, sums, far_in, y_in, cols_sum, packed, dom_in,
        load_sem, own_sem, tab_sem, a_send, a_recv, y_send, y_recv, f_send, f_recv, p_send, p_recv,
        c_send, c_recv, s_send, s_recv, h_send, h_recv, d_send, d_recv):
    d = lax.axis_index("dom")
    r = lax.axis_index("rep")
    z, x = d // xs_n, lax.rem(d, xs_n)
    y, c = r // 2, lax.rem(r, 2)
    peers = zs_n * xs_n
    slot_rows = 4
    piece = 2 * ys_n * slot_rows
    side = edge_ref.shape[1]
    r_up = wrap(y + 1, ys_n) * 2 + c
    r_down = wrap(y - 1, ys_n) * 2 + c
    r_far = wrap(y + 2, ys_n) * 2 + c
    r_pair = r + 1 - 2 * c
    r_way = (r_up, r_down)
    group = peers // 2
    home = d // group
    bf16, f32 = jnp.bfloat16, jnp.float32

    def offset(j):
        return ((j + 1) // 2) * (2 * lax.rem(j, 2) - 1)

    loads = [pltpu.make_async_copy(a, b, load_sem.at[n]) for n, (a, b) in enumerate((
        (perm_hbm, perm_ref), (grad_hbm, grad_ref), (index_hbm, index_ref),
        (edge_hbm, edge_ref), (feat_hbm, feat_ref), (weight_hbm, weight_ref)))]
    for load in loads:
        load.start()

    barrier = pltpu.get_barrier_semaphore()

    @pl.loop(1, peers)
    def _(n):
        pl.semaphore_signal(barrier, inc=1, device_id={"dom": wrap(d + n, peers), "rep": r},
                            device_id_type=MESH)

    for other in (*r_way, r_pair):
        pl.semaphore_signal(barrier, inc=1, device_id={"dom": d, "rep": other},
                            device_id_type=MESH)

    @pl.when(c != home)
    def _():
        @pl.loop(0, peers)
        def _(n):
            pl.semaphore_signal(barrier, inc=1,
                                device_id={"dom": wrap(d + n, peers), "rep": r_pair},
                                device_id_type=MESH)

    loads[0].wait()
    perm = perm_ref[...]
    target = (perm // grad_ref.shape[0]) * slot_rows + lax.rem(perm, slot_rows)
    tile = 256
    loads[1].wait()

    @pl.loop(0, grad_ref.shape[0] // tile)
    def _(t):
        rows = lax.broadcasted_iota(jnp.int32, (tile, grad_ref.shape[0]), 0) + t * tile
        hot = jnp.where(rows == target, 1.0, 0.0).astype(bf16)
        ordered[pl.ds(pl.multiple_of(t * tile, tile), tile), :] = lax.dot_general(
            hot, grad_ref[...], (((1,), (0,)), ((), ())), preferred_element_type=f32).astype(bf16)

    loads[2].wait()
    table_ref[...] = make_table(index_ref[...], count_ref[0])
    tab_copy = pltpu.make_async_copy(table_ref, tab, tab_sem)
    tab_copy.start()
    q = lax.broadcasted_iota(jnp.int32, (tile, tile), 0)
    p = lax.broadcasted_iota(jnp.int32, (tile, tile), 1)
    wanted = lax.rem(q // slot_rows, 8) * piece + (q // piece) * slot_rows + lax.rem(q, slot_rows)
    unperm[...] = jnp.where(p == wanted, 1.0, 0.0).astype(bf16)

    pl.semaphore_wait(barrier, peers - 1 + 3 + group)

    own = pltpu.make_async_copy(
        ordered.at[pl.ds(pl.multiple_of(d * piece, piece), piece)], raw.at[z, x, r], own_sem)
    own.start()

    def a_copy(n, zs, xs):
        j, i = n // xs_n, lax.rem(n, xs_n)
        to = wrap(z + offset(j), zs_n) * xs_n + wrap(x + i, xs_n)
        return pltpu.make_async_remote_copy(
            src_ref=ordered.at[pl.ds(pl.multiple_of(to * piece, piece), piece)],
            dst_ref=raw.at[zs, xs, r],
            send_sem=a_send.at[n], recv_sem=a_recv.at[n],
            device_id={"dom": to, "rep": r}, device_id_type=MESH)

    @pl.loop(1, peers)
    def _(n):
        a_copy(n, z, x).start()

    def chunk_of(j):
        return wrap(z - offset(j), zs_n)

    def y_copy(j, way, owner):
        part = raw.at[chunk_of(j), :, owner]
        return pltpu.make_async_remote_copy(
            src_ref=part, dst_ref=part, send_sem=y_send.at[way, j], recv_sem=y_recv.at[way, j],
            device_id={"dom": d, "rep": r_way[way]}, device_id_type=MESH)

    half = xs_n // 2

    def f_copy(j, way, owner):
        part = raw.at[chunk_of(j), pl.ds(way * half, half), owner]
        return pltpu.make_async_remote_copy(
            src_ref=part, dst_ref=part, send_sem=f_send.at[way, j], recv_sem=f_recv.at[way, j],
            device_id={"dom": d, "rep": r_way[way]}, device_id_type=MESH)

    def p_copy(j, which, owner):
        part = raw.at[chunk_of(j), :, owner]
        return pltpu.make_async_remote_copy(
            src_ref=part, dst_ref=part, send_sem=p_send.at[which, j],
            recv_sem=p_recv.at[which, j],
            device_id={"dom": d, "rep": r_pair}, device_id_type=MESH)

    quarter = edge_ref.shape[0] // 4

    def sum_pairs(part):
        @pl.loop(0, quarter)
        def _(n):
            at = part * quarter + n
            slot = jnp.clip(tab[0, at], 0, edge_ref.shape[0] - 1)
            total = jnp.where(tab[1, at] > 0, running[...], 0.0) + edge_ref[slot].astype(f32)
            running[...] = total
            summed[at] = total.T.astype(bf16)

    loads[3].wait()
    tab_copy.wait()
    running[...] = jnp.zeros_like(running)
    summed[edge_ref.shape[0]] = jnp.zeros((side, side), bf16)
    sum_pairs(0)
    acc[...] = jnp.zeros_like(acc)

    @pl.loop(0, zs_n + 3)
    def _(step):
        @pl.when(step < zs_n)
        def _():
            j = step

            @pl.when(j == 0)
            def _():
                own.wait()

            @pl.loop(0, xs_n)
            def _(i):
                @pl.when(j * xs_n + i > 0)
                def _():
                    a_copy(j * xs_n + i, chunk_of(j), wrap(x - i, xs_n)).wait_recv()

            y_copy(j, 0, r).start()
            y_copy(j, 1, r).start()
            p_copy(j, 0, r).start()

        @pl.when((step >= 1) & (step < zs_n + 1))
        def _():
            j = step - 1
            y_copy(j, 0, r_down).wait_recv()
            f_copy(j, 0, r_down).start()
            p_copy(j, 1, r_down).start()
            y_copy(j, 1, r_up).wait_recv()
            f_copy(j, 1, r_up).start()
            p_copy(j, 2, r_up).start()

        @pl.when((step >= 2) & (step < zs_n + 2))
        def _():
            j = step - 2
            f_copy(j, 0, r_far).wait_recv()
            f_copy(j, 1, r_far).wait_recv()
            p_copy(j, 3, r_far).start()

        @pl.when(step < 3)
        def _():
            sum_pairs(step + 1)

        @pl.when(step >= 3)
        def _():
            j = step - 3
            zs = chunk_of(j)
            for t in range(8):
                for col in range(8):
                    pair = t * 64 + zs * 8 + col
                    place = tab[2 + pair // side, lax.rem(pair, side)]
                    dense[col * side:(col + 1) * side, t * side:(t + 1) * side] = summed[
                        jnp.clip(place, 0, edge_ref.shape[0])]
            flip = 1 - 2 * c
            p_copy(j, 0, r + flip).wait_recv()
            p_copy(j, 1, r_down + flip).wait_recv()
            p_copy(j, 2, r_up + flip).wait_recv()
            p_copy(j, 3, r_far + flip).wait_recv()
            for xs in range(xs_n):
                rows = raw[zs, xs].reshape(tile, acc.shape[1])
                placed = lax.dot_general(
                    unperm[...], rows, (((1,), (0,)), ((), ())),
                    preferred_element_type=f32).astype(bf16)
                for t in range(2 * ys_n):
                    chunk[t * side + xs * piece:t * side + (xs + 1) * piece, :] = placed[
                        t * piece:(t + 1) * piece, :]
            acc[...] += lax.dot_general(
                dense[...], chunk[...], (((1,), (0,)), ((), ())), preferred_element_type=f32)

    agg_ref[...] = acc[...].astype(bf16)
    for load in loads[4:]:
        load.wait()
    out_rows = out_ref.shape[0]
    tall, lanes = cols_sum.shape
    mid = tall // 2

    def partial(half):
        cols = feat_ref[:, pl.ds(pl.multiple_of(half * tall, tall), tall)]
        return lax.dot_general(
            cols, agg_ref[...], (((0,), (0,)), ((), ())),
            preferred_element_type=jnp.float32) * scale

    part_other[...] = partial(1 - c)

    def wide(n):
        return pl.ds(pl.multiple_of(wrap(y + n, ys_n) * lanes, lanes), lanes)

    def c_copy(n):
        return pltpu.make_async_remote_copy(
            src_ref=part_other.at[:, wide(n)], dst_ref=pair_in.at[n],
            send_sem=c_send.at[n], recv_sem=c_recv.at[n],
            device_id={"dom": d, "rep": r_pair}, device_id_type=MESH)

    def s_copy(way):
        return pltpu.make_async_remote_copy(
            src_ref=sums.at[2, pl.ds(way * mid, mid)], dst_ref=far_in.at[way],
            send_sem=s_send.at[way], recv_sem=s_recv.at[way],
            device_id={"dom": d, "rep": r_way[way]}, device_id_type=MESH)

    def h_copy(way, part):
        place = pl.ds(part * mid, mid)
        return pltpu.make_async_remote_copy(
            src_ref=sums.at[1 + 2 * way, place], dst_ref=y_in.at[way, place],
            send_sem=h_send.at[way, part], recv_sem=h_recv.at[way, part],
            device_id={"dom": d, "rep": r_way[way]}, device_id_type=MESH)

    def add_pair(n):
        c_copy(n).wait_recv()
        sums[n] = part_mine[:, wide(n)] + pair_in[n]

    for n in (2, 1, 3, 0):
        c_copy(n).start()
    part_mine[...] = partial(c)
    add_pair(2)
    for way in range(2):
        s_copy(way).start()
    for way in range(2):
        add_pair(1 + 2 * way)
        h_copy(way, 1 - way).start()
    add_pair(0)
    for way in range(2):
        s_copy(way).wait_recv()
        sums[1 + 2 * way, way * mid:(way + 1) * mid] += far_in[way]
        h_copy(way, way).start()
    for way in range(2):
        h_copy(way, 1 - way).wait_recv()
    for way in range(2):
        h_copy(way, way).wait_recv()
    cols_sum[...] = sums[0] + (y_in[0] + y_in[1])
    both = cols_sum[...].reshape(group, out_rows, lanes)
    low, high = both[:, :out_rows // 2], both[:, out_rows // 2:]
    left = lax.broadcasted_iota(jnp.int32, low.shape, 2) < lanes // 2
    packed[0] = jnp.where(left, low, pltpu.roll(high, lanes // 2, 2))
    packed[1] = jnp.where(left, pltpu.roll(low, lanes // 2, 2), high)

    def d_copy(n, core):
        return pltpu.make_async_remote_copy(
            src_ref=packed.at[core, n], dst_ref=dom_in.at[d],
            send_sem=d_send.at[core, n], recv_sem=d_recv.at[d],
            device_id={"dom": c * group + n, "rep": y * 2 + core}, device_id_type=MESH)

    @pl.loop(0, group)
    def _(m):
        n = lax.rem(m + d + group // 2, group)
        for core in range(2):
            @pl.when((c * group + n != d) | (c != core))
            def _():
                d_copy(n, core).start()

    gi_ref[...] = lax.dot_general(
        agg_ref[...], weight_ref[...], (((1,), (1,)), ((), ())),
        preferred_element_type=f32).astype(gi_ref.dtype)

    @pl.when(c == home)
    def _():
        dom_in[d] = packed[c, d - c * group]

    @pl.loop(0, peers)
    def _(s):
        @pl.when((s != d) | (c != home))
        def _():
            pltpu.make_async_remote_copy(
                src_ref=packed.at[0, 0], dst_ref=dom_in.at[s],
                send_sem=d_send.at[0, 0], recv_sem=d_recv.at[s],
                device_id={"dom": d, "rep": r_pair}, device_id_type=MESH).wait_recv()

    sums_of = [dom_in[s] for s in range(peers)]
    while len(sums_of) > 1:
        sums_of = [a + b for a, b in zip(sums_of[::2], sums_of[1::2])]
    total = sums_of[0]
    out_ref[:out_rows // 2] = total[:, :lanes // 2]
    out_ref[out_rows // 2:] = total[:, lanes // 2:]

    for n in range(ys_n):
        c_copy(n).wait_send()
    for way in range(2):
        s_copy(way).wait_send()
        for part in range(2):
            h_copy(way, part).wait_send()
    @pl.loop(0, group)
    def _(n):
        for core in range(2):
            @pl.when((c * group + n != d) | (c != core))
            def _():
                d_copy(n, core).wait_send()

    @pl.loop(1, peers)
    def _(n):
        a_copy(n, z, x).wait_send()

    @pl.loop(0, zs_n)
    def _(j):
        for way in range(2):
            y_copy(j, way, r).wait_send()
            f_copy(j, way, r).wait_send()
        for which in range(4):
            p_copy(j, which, r).wait_send()


def layer(perm, grad, index, count, edge, feat, weight, scale):
    zs_n, xs_n, ys_n = SIZES
    rows, width = grad.shape
    fin = feat.shape[1]
    reps, doms = 2 * ys_n, zs_n * xs_n
    piece = rows // doms
    slots, side = edge.shape[0], edge.shape[1]
    tall, lanes = fin // 2, width // ys_n
    out_rows = fin // doms
    far = pl.BlockSpec(memory_space=pltpu.HBM)
    vmem = pl.BlockSpec(memory_space=pltpu.VMEM)
    dma = pltpu.SemaphoreType.DMA
    f32, bf16 = jnp.float32, grad.dtype
    args = (perm.reshape(1, rows), grad, index, count, edge, feat, weight)
    args = tuple(a if n == 3 else pltpu.with_memory_space_constraint(a, pltpu.HBM)
                 for n, a in enumerate(args))
    return pl.pallas_call(
        lambda *refs: layer_kernel(zs_n, xs_n, ys_n, scale, *refs),
        out_shape=(jax.ShapeDtypeStruct((rows, fin), bf16),
                   jax.ShapeDtypeStruct((out_rows, lanes // 2), f32)),
        in_specs=[far] * 3 + [pl.BlockSpec(memory_space=pltpu.SMEM)] + [far] * 3,
        out_specs=(vmem, vmem),
        scratch_shapes=[
            pltpu.VMEM((1, rows), jnp.int32),
            pltpu.VMEM(grad.shape, bf16),
            pltpu.VMEM(index.shape, jnp.int32),
            pltpu.VMEM(edge.shape, bf16),
            pltpu.VMEM(feat.shape, bf16),
            pltpu.VMEM(weight.shape, bf16),
            pltpu.VMEM((rows, width), bf16),
            pltpu.VMEM((zs_n, xs_n, reps, piece, width), bf16),
            pltpu.VMEM((256, 256), bf16),
            pltpu.VMEM((8, slots), jnp.int32),
            pltpu.SMEM((8, slots), jnp.int32),
            pltpu.VMEM((side, side), f32),
            pltpu.VMEM((slots + 1, side, side), bf16),
            pltpu.VMEM((rows, rows), bf16),
            pltpu.VMEM((rows, width), bf16),
            pltpu.VMEM((rows, width), f32),
            pltpu.VMEM((rows, width), bf16),
            pltpu.VMEM((tall, width), f32), pltpu.VMEM((tall, width), f32),
            pltpu.VMEM((ys_n, tall, lanes), f32), pltpu.VMEM((ys_n, tall, lanes), f32),
            pltpu.VMEM((2, tall // 2, lanes), f32), pltpu.VMEM((2, tall, lanes), f32),
            pltpu.VMEM((tall, lanes), f32),
            pltpu.VMEM((2, doms // 2, out_rows // 2, lanes), f32),
            pltpu.VMEM((doms, out_rows // 2, lanes), f32),
            dma((6,)), dma, dma, dma((doms,)), dma((doms,)),
            dma((2, zs_n)), dma((2, zs_n)), dma((2, zs_n)), dma((2, zs_n)),
            dma((4, zs_n)), dma((4, zs_n)),
            dma((ys_n,)), dma((ys_n,)), dma((2,)), dma((2,)), dma((2, 2)), dma((2, 2)),
            dma((2, doms // 2)), dma((doms,)),
        ],
        compiler_params=pltpu.CompilerParams(
            collective_id=0, has_side_effects=True, vmem_limit_bytes=56 << 20),
        name="layer",
    )(*args)


def on_device(grad_out, features, weight, edge_blocks, block_index, block_count, node_perm):
    nodes = grad_out.shape[0] * lax.axis_size("dom") * lax.axis_size("rep")
    return layer(node_perm, grad_out, block_index.T, block_count, edge_blocks, features, weight,
                 1.0 / math.sqrt(nodes))


def solution(mesh):
    in_specs = (
        P(("dom", "rep"), None),
        P(("dom", "rep"), None),
        P(),
        P(("dom", "rep"), None, None),
        P(("dom", "rep"), None),
        P(("dom", "rep")),
        P(("dom", "rep")),
    )
    out_specs = (P(("dom", "rep"), None), P("dom", "rep"))
    return jax.shard_map(
        on_device, mesh=mesh, in_specs=in_specs, out_specs=out_specs, check_vma=False
    )
```

time: 125 us -> 90.7 us (0.73); the launches traced: 124 us -> 90.6 us
  Pallas kernels: 114 us -> 85.8 us
  local copies, waits for them, and re-layouts: 8.33 us -> 3.56 us
    pallas_call x3 -> x1, Pallas kernels: 114 us -> 85.8 us  [layer(): pl.pallas_call(lambda *refs: layer_kernel(zs_n, xs_n, ys_n, scale, *refs)...]
    unnamed x16 -> x2, local copies, waits for them, and re-layouts: 8.2 us -> 3.56 us
where the time goes in v5:
time: 90.7 us; the launch traced here: 90.6 us
  Pallas kernels  85.8 us (95%)
  local copies, waits for them, and re-layouts  3.56 us (4%)
  between operations  1.29 us (1%)
    pallas_call x1, Pallas kernels, layer(): pl.pallas_call(lambda *refs: layer_kernel(zs_n, xs_n, ys_n, scale, *refs)...  85.8 us
    unnamed x2, local copies, waits for them, and re-layouts  3.56 us

profile of v5, /device:TPU:1, one launch (start us, length us, event | category | flops | bytes accessed | tf_op | source)
XLA Modules:
  0.0 90.6 jit_solution(11248295434042917987)
XLA Ops:
  1.3 85.8 %layer.1 = (bf16[1024,512]{1,0:T(8,128)(2,1)}, f32[16,64]{1,0:T(8,128)}) custom-call(s32[1,1024]{1,0:T(1,128)} %bitcast.2, bf16[1024,512]{1,0:T(8,128)(2,1)} %refs_1_.1, s32[2,128]{1,0:T(2,128)} %bitcast.3, s32[1]{0:T(128)S(6)} %copy.11.refs_3_, bf16[128,128,128]{2,1,0:T(8,128)(2,1)} %refs_4_.1, bf16[1024,512]{1,0:T(8,128)(2,1)} %refs_5_.1, ...), custom_call_target="tpu_custom_call" | custom-call | tf_op jit(solution)/shard_map/layer/pallas_call | solution.py:395
  87.0 2.3 %copy.12 = bf16[1024,512]{1,0:T(8,128)(2,1)} copy(bf16[1024,512]{1,0:T(8,128)(2,1)} %get-tuple-element.4) | data formatting | bytes 2097152
  89.3 1.3 %copy.13 = f32[16,64]{1,0:T(8,128)} copy(f32[16,64]{1,0:T(8,128)} %get-tuple-element.5) | data formatting | bytes 8192

commit v6 on v5

--- a/solution.py
+++ b/solution.py
@@ -44,10 +44,10 @@
 
 def layer_kernel(
         zs_n, xs_n, ys_n, scale,
-        perm_hbm, grad_hbm, index_hbm, count_ref, edge_hbm, feat_hbm, weight_hbm,
-        gi_ref, out_ref,
-        perm_ref, grad_ref, index_ref, edge_ref, feat_ref, weight_ref, ordered, raw, unperm,
-        table_ref, tab, running, summed, dense, chunk, acc, agg_ref,
+        perm_hbm, grad_hbm, index_hbm, count_ref, edge_hbm, feat_hbm,
+        agg_ref, out_ref,
+        perm_ref, grad_ref, index_ref, edge_ref, feat_ref, ordered, raw, unperm,
+        table_ref, tab, running, summed, dense, chunk, acc,
         part_other, part_mine, pair_in, sums, far_in, y_in, cols_sum, packed, dom_in,
         load_sem, own_sem, tab_sem, a_send, a_recv, y_send, y_recv, f_send, f_recv, p_send, p_recv,
         c_send, c_recv, s_send, s_recv, h_send, h_recv, d_send, d_recv):
@@ -73,8 +73,8 @@
 
     loads = [pltpu.make_async_copy(a, b, load_sem.at[n]) for n, (a, b) in enumerate((
         (perm_hbm, perm_ref), (grad_hbm, grad_ref), (index_hbm, index_ref),
-        (edge_hbm, edge_ref), (feat_hbm, feat_ref), (weight_hbm, weight_ref)))]
-    for load in loads:
+        (edge_hbm, edge_ref), (feat_hbm, feat_ref)))]
+    for load in loads[:3]:
         load.start()
 
     barrier = pltpu.get_barrier_semaphore()
@@ -101,6 +101,8 @@
     target = (perm // grad_ref.shape[0]) * slot_rows + lax.rem(perm, slot_rows)
     tile = 256
     loads[1].wait()
+    for load in loads[3:]:
+        load.start()
 
     @pl.loop(0, grad_ref.shape[0] // tile)
     def _(t):
@@ -172,6 +174,19 @@
             running[...] = total
             summed[at] = total.T.astype(bf16)
 
+    def send_own(j):
+        @pl.loop(0, xs_n)
+        def _(i):
+            @pl.when(j * xs_n + i > 0)
+            def _():
+                a_copy(j * xs_n + i, chunk_of(j), wrap(x - i, xs_n)).wait_recv()
+
+        y_copy(j, 0, r).start()
+        y_copy(j, 1, r).start()
+        p_copy(j, 0, r).start()
+
+    own.wait()
+    send_own(0)
     loads[3].wait()
     tab_copy.wait()
     running[...] = jnp.zeros_like(running)
@@ -181,23 +196,9 @@
 
     @pl.loop(0, zs_n + 3)
     def _(step):
-        @pl.when(step < zs_n)
-        def _():
-            j = step
-
-            @pl.when(j == 0)
-            def _():
-                own.wait()
-
-            @pl.loop(0, xs_n)
-            def _(i):
-                @pl.when(j * xs_n + i > 0)
-                def _():
-                    a_copy(j * xs_n + i, chunk_of(j), wrap(x - i, xs_n)).wait_recv()
-
-            y_copy(j, 0, r).start()
-            y_copy(j, 1, r).start()
-            p_copy(j, 0, r).start()
+        @pl.when(step + 1 < zs_n)
+        def _():
+            send_own(step + 1)
 
         @pl.when((step >= 1) & (step < zs_n + 1))
         def _():
@@ -326,10 +327,6 @@
             def _():
                 d_copy(n, core).start()
 
-    gi_ref[...] = lax.dot_general(
-        agg_ref[...], weight_ref[...], (((1,), (1,)), ((), ())),
-        preferred_element_type=f32).astype(gi_ref.dtype)
-
     @pl.when(c == home)
     def _():
         dom_in[d] = packed[c, d - c * group]
@@ -376,7 +373,7 @@
             p_copy(j, which, r).wait_send()
 
 
-def layer(perm, grad, index, count, edge, feat, weight, scale):
+def layer(perm, grad, index, count, edge, feat, scale):
     zs_n, xs_n, ys_n = SIZES
     rows, width = grad.shape
     fin = feat.shape[1]
@@ -389,14 +386,14 @@
     vmem = pl.BlockSpec(memory_space=pltpu.VMEM)
     dma = pltpu.SemaphoreType.DMA
     f32, bf16 = jnp.float32, grad.dtype
-    args = (perm.reshape(1, rows), grad, index, count, edge, feat, weight)
+    args = (perm.reshape(1, rows), grad, index, count, edge, feat)
     args = tuple(a if n == 3 else pltpu.with_memory_space_constraint(a, pltpu.HBM)
                  for n, a in enumerate(args))
     return pl.pallas_call(
         lambda *refs: layer_kernel(zs_n, xs_n, ys_n, scale, *refs),
-        out_shape=(jax.ShapeDtypeStruct((rows, fin), bf16),
+        out_shape=(jax.ShapeDtypeStruct((rows, width), bf16),
                    jax.ShapeDtypeStruct((out_rows, lanes // 2), f32)),
-        in_specs=[far] * 3 + [pl.BlockSpec(memory_space=pltpu.SMEM)] + [far] * 3,
+        in_specs=[far] * 3 + [pl.BlockSpec(memory_space=pltpu.SMEM)] + [far] * 2,
         out_specs=(vmem, vmem),
         scratch_shapes=[
             pltpu.VMEM((1, rows), jnp.int32),
@@ -404,7 +401,6 @@
             pltpu.VMEM(index.shape, jnp.int32),
             pltpu.VMEM(edge.shape, bf16),
             pltpu.VMEM(feat.shape, bf16),
-            pltpu.VMEM(weight.shape, bf16),
             pltpu.VMEM((rows, width), bf16),
             pltpu.VMEM((zs_n, xs_n, reps, piece, width), bf16),
             pltpu.VMEM((256, 256), bf16),
@@ -415,29 +411,54 @@
             pltpu.VMEM((rows, rows), bf16),
             pltpu.VMEM((rows, width), bf16),
             pltpu.VMEM((rows, width), f32),
-            pltpu.VMEM((rows, width), bf16),
             pltpu.VMEM((tall, width), f32), pltpu.VMEM((tall, width), f32),
             pltpu.VMEM((ys_n, tall, lanes), f32), pltpu.VMEM((ys_n, tall, lanes), f32),
             pltpu.VMEM((2, tall // 2, lanes), f32), pltpu.VMEM((2, tall, lanes), f32),
             pltpu.VMEM((tall, lanes), f32),
             pltpu.VMEM((2, doms // 2, out_rows // 2, lanes), f32),
             pltpu.VMEM((doms, out_rows // 2, lanes), f32),
-            dma((6,)), dma, dma, dma((doms,)), dma((doms,)),
+            dma((5,)), dma, dma, dma((doms,)), dma((doms,)),
             dma((2, zs_n)), dma((2, zs_n)), dma((2, zs_n)), dma((2, zs_n)),
             dma((4, zs_n)), dma((4, zs_n)),
             dma((ys_n,)), dma((ys_n,)), dma((2,)), dma((2,)), dma((2, 2)), dma((2, 2)),
             dma((2, doms // 2)), dma((doms,)),
         ],
         compiler_params=pltpu.CompilerParams(
-            collective_id=0, has_side_effects=True, vmem_limit_bytes=56 << 20),
+            collective_id=0, has_side_effects=True, vmem_limit_bytes=48 << 20),
         name="layer",
     )(*args)
 
 
+def finish_kernel(agg_ref, weight_ref, sum_ref, gi_ref, out_ref):
+    gi_ref[...] = lax.dot_general(
+        agg_ref[...], weight_ref[...], (((1,), (1,)), ((), ())),
+        preferred_element_type=jnp.float32).astype(gi_ref.dtype)
+    out_ref[...] = sum_ref[...]
+
+
+def finish(agg, weight, summed):
+    rows, width = agg.shape
+    tile = 256
+    whole = pl.BlockSpec(summed.shape, lambda i: (0, 0))
+    return pl.pallas_call(
+        finish_kernel,
+        grid=(rows // tile,),
+        out_shape=(jax.ShapeDtypeStruct((rows, weight.shape[0]), agg.dtype),
+                   jax.ShapeDtypeStruct(summed.shape, summed.dtype)),
+        in_specs=[pl.BlockSpec((tile, width), lambda i: (i, 0)),
+                  pl.BlockSpec(weight.shape, lambda i: (0, 0)), whole],
+        out_specs=(pl.BlockSpec((tile, weight.shape[0]), lambda i: (i, 0)), whole),
+        compiler_params=pltpu.CompilerParams(vmem_limit_bytes=8 << 20),
+        name="finish",
+    )(agg, weight, summed)
+
+
 def on_device(grad_out, features, weight, edge_blocks, block_index, block_count, node_perm):
     nodes = grad_out.shape[0] * lax.axis_size("dom") * lax.axis_size("rep")
-    return layer(node_perm, grad_out, block_index.T, block_count, edge_blocks, features, weight,
-                 1.0 / math.sqrt(nodes))
+    aggregated, summed = layer(
+        node_perm, grad_out, block_index.T, block_count, edge_blocks, features,
+        1.0 / math.sqrt(nodes))
+    return finish(aggregated, weight, summed)
 
 
 def solution(mesh):

time: 90.7 us -> 89.6 us (0.988)
  local copies, waits for them, and re-layouts: 3.56 us -> 0.01 us
  Pallas kernels: 85.8 us -> 88.2 us
    unnamed x2, local copies, waits for them, and re-layouts: 3.56 us -> 0.01 us
    pallas_call x0 -> x1, Pallas kernels: none -> 2.44 us  [finish(): pl.pallas_call(finish_kernel, grid=(rows // tile,), out_shape=(jax.ShapeD...]
where the time goes in v6:
time: 89.6 us; the launch traced here: 89.5 us
  Pallas kernels  88.2 us (98%)
  between operations  1.36 us (2%)
    pallas_call x1, Pallas kernels, layer(): pl.pallas_call(lambda *refs: layer_kernel(zs_n, xs_n, ys_n, scale, *refs)...  85.7 us
    pallas_call x1, Pallas kernels, finish(): pl.pallas_call(finish_kernel, grid=(rows // tile,), out_shape=(jax.ShapeD...  2.44 us

profile of v6, /device:TPU:1, one launch (start us, length us, event | category | flops | bytes accessed | tf_op | source)
XLA Modules:
  0.0 89.5 jit_solution(4461898918478088709)
XLA Ops:
  0.6 0.0 copy-start
  1.3 85.7 %layer.1 = (bf16[1024,512]{1,0:T(8,128)(2,1)S(1)}, f32[16,64]{1,0:T(8,128)S(1)}) custom-call(s32[1,1024]{1,0:T(1,128)} %bitcast.2, bf16[1024,512]{1,0:T(8,128)(2,1)} %refs_1_.1, s32[2,128]{1,0:T(2,128)} %bitcast.3, s32[1]{0:T(128)S(6)} %copy.9.refs_3_, bf16[128,128,128]{2,1,0:T(8,128)(2,1)} %refs_4_.1, bf16[1024,512]{1,0:T(8,128)(2,1)} %refs_5_.1), custom_call_target="tpu_custom_call" | custom-call | tf_op jit(solution)/shard_map/layer/pallas_call | solution.py:392
  87.1 0.0 copy-done
  87.1 2.4 %finish.1 = (bf16[1024,512]{1,0:T(8,128)(2,1)}, f32[16,64]{1,0:T(8,128)}) custom-call(bf16[1024,512]{1,0:T(8,128)(2,1)S(1)} %get-tuple-element.4.agg_ref, bf16[512,512]{1,0:T(8,128)(2,1)S(1)} %copy-done, f32[16,64]{1,0:T(8,128)S(1)} %get-tuple-element.5.sum_ref), custom_call_target="tpu_custom_call" | custom-call | tf_op jit(solution)/shard_map/finish/pallas_call | solution.py:443
Async XLA Ops:
  0.6 86.4 %copy-start = (bf16[512,512]{1,0:T(8,128)(2,1)S(1)}, bf16[512,512]{1,0:T(8,128)(2,1)}, u32[]{:S(2)}) copy-start(bf16[512,512]{1,0:T(8,128)(2,1)} %weight_ref.1) | copy-start | bytes 1572868

commit v7 on v5

--- a/solution.py
+++ b/solution.py
@@ -44,8 +44,8 @@
 
 def layer_kernel(
         zs_n, xs_n, ys_n, scale,
-        perm_hbm, grad_hbm, index_hbm, count_ref, edge_hbm, feat_hbm, weight_hbm,
-        gi_ref, out_ref,
+        perm_hbm, grad_hbm, index_hbm, count_ref, edge_hbm, feat_hbm,
+        weight_hbm, gi_ref, out_ref,
         perm_ref, grad_ref, index_ref, edge_ref, feat_ref, weight_ref, ordered, raw, unperm,
         table_ref, tab, running, summed, dense, chunk, acc, agg_ref,
         part_other, part_mine, pair_in, sums, far_in, y_in, cols_sum, packed, dom_in,
@@ -74,7 +74,7 @@
     loads = [pltpu.make_async_copy(a, b, load_sem.at[n]) for n, (a, b) in enumerate((
         (perm_hbm, perm_ref), (grad_hbm, grad_ref), (index_hbm, index_ref),
         (edge_hbm, edge_ref), (feat_hbm, feat_ref), (weight_hbm, weight_ref)))]
-    for load in loads:
+    for load in loads[:3]:
         load.start()
 
     barrier = pltpu.get_barrier_semaphore()
@@ -101,6 +101,8 @@
     target = (perm // grad_ref.shape[0]) * slot_rows + lax.rem(perm, slot_rows)
     tile = 256
     loads[1].wait()
+    for load in loads[3:]:
+        load.start()
 
     @pl.loop(0, grad_ref.shape[0] // tile)
     def _(t):
@@ -172,6 +174,19 @@
             running[...] = total
             summed[at] = total.T.astype(bf16)
 
+    def send_own(j):
+        @pl.loop(0, xs_n)
+        def _(i):
+            @pl.when(j * xs_n + i > 0)
+            def _():
+                a_copy(j * xs_n + i, chunk_of(j), wrap(x - i, xs_n)).wait_recv()
+
+        y_copy(j, 0, r).start()
+        y_copy(j, 1, r).start()
+        p_copy(j, 0, r).start()
+
+    own.wait()
+    send_own(0)
     loads[3].wait()
     tab_copy.wait()
     running[...] = jnp.zeros_like(running)
@@ -181,23 +196,9 @@
 
     @pl.loop(0, zs_n + 3)
     def _(step):
-        @pl.when(step < zs_n)
-        def _():
-            j = step
-
-            @pl.when(j == 0)
-            def _():
-                own.wait()
-
-            @pl.loop(0, xs_n)
-            def _(i):
-                @pl.when(j * xs_n + i > 0)
-                def _():
-                    a_copy(j * xs_n + i, chunk_of(j), wrap(x - i, xs_n)).wait_recv()
-
-            y_copy(j, 0, r).start()
-            y_copy(j, 1, r).start()
-            p_copy(j, 0, r).start()
+        @pl.when(step + 1 < zs_n)
+        def _():
+            send_own(step + 1)
 
         @pl.when((step >= 1) & (step < zs_n + 1))
         def _():
@@ -208,13 +209,6 @@
             y_copy(j, 1, r_up).wait_recv()
             f_copy(j, 1, r_up).start()
             p_copy(j, 2, r_up).start()
-
-        @pl.when((step >= 2) & (step < zs_n + 2))
-        def _():
-            j = step - 2
-            f_copy(j, 0, r_far).wait_recv()
-            f_copy(j, 1, r_far).wait_recv()
-            p_copy(j, 3, r_far).start()
 
         @pl.when(step < 3)
         def _():
@@ -245,6 +239,13 @@
                         t * piece:(t + 1) * piece, :]
             acc[...] += lax.dot_general(
                 dense[...], chunk[...], (((1,), (0,)), ((), ())), preferred_element_type=f32)
+
+        @pl.when((step >= 2) & (step < zs_n + 2))
+        def _():
+            j = step - 2
+            f_copy(j, 0, r_far).wait_recv()
+            f_copy(j, 1, r_far).wait_recv()
+            p_copy(j, 3, r_far).start()
 
     agg_ref[...] = acc[...].astype(bf16)
     for load in loads[4:]:
@@ -429,7 +430,7 @@
             dma((2, doms // 2)), dma((doms,)),
         ],
         compiler_params=pltpu.CompilerParams(
-            collective_id=0, has_side_effects=True, vmem_limit_bytes=56 << 20),
+            collective_id=0, has_side_effects=True, vmem_limit_bytes=46 << 20),
         name="layer",
     )(*args)
 

time: 90.7 us -> 85.1 us (0.938)
  Pallas kernels: 85.8 us -> 82.2 us
  local copies, waits for them, and re-layouts: 3.56 us -> 1.57 us
    pallas_call x1, Pallas kernels: 85.8 us -> 82.2 us  [layer(): pl.pallas_call(lambda *refs: layer_kernel(zs_n, xs_n, ys_n, scale, *refs)...]
    unnamed x2, local copies, waits for them, and re-layouts: 3.56 us -> 1.57 us
where the time goes in v7:
time: 85.1 us; the launch traced here: 85 us
  Pallas kernels  82.2 us (97%)
  local copies, waits for them, and re-layouts  1.57 us (2%)
  between operations  1.29 us (2%)
    pallas_call x1, Pallas kernels, layer(): pl.pallas_call(lambda *refs: layer_kernel(zs_n, xs_n, ys_n, scale, *refs)...  82.2 us

profile of v7, /device:TPU:1, one launch (start us, length us, event | category | flops | bytes accessed | tf_op | source)
XLA Modules:
  0.0 85.0 jit_solution(9178338085567563155)
XLA Ops:
  1.3 82.2 %layer.1 = (bf16[1024,512]{1,0:T(8,128)(2,1)S(1)}, f32[16,64]{1,0:T(8,128)S(1)}) custom-call(s32[1,1024]{1,0:T(1,128)} %bitcast.2, bf16[1024,512]{1,0:T(8,128)(2,1)} %refs_1_.1, s32[2,128]{1,0:T(2,128)} %bitcast.3, s32[1]{0:T(128)S(6)} %copy.11.refs_3_, bf16[128,128,128]{2,1,0:T(8,128)(2,1)} %refs_4_.1, bf16[1024,512]{1,0:T(8,128)(2,1)} %refs_5_.1, ...), custom_call_target="tpu_custom_call" | custom-call | tf_op jit(solution)/shard_map/layer/pallas_call | solution.py:396
  83.4 1.0 %copy.12 = bf16[1024,512]{1,0:T(8,128)(2,1)} copy(bf16[1024,512]{1,0:T(8,128)(2,1)S(1)} %get-tuple-element.4) | data formatting | bytes 2097152
  84.4 0.6 copy.13

commit v8 on v7

--- a/solution.py
+++ b/solution.py
@@ -79,9 +79,10 @@
 
     barrier = pltpu.get_barrier_semaphore()
 
-    @pl.loop(1, peers)
+    @pl.loop(0, peers - 1)
     def _(n):
-        pl.semaphore_signal(barrier, inc=1, device_id={"dom": wrap(d + n, peers), "rep": r},
+        to = wrap(d + 1 + lax.rem(n + peers // 2 - 4, peers - 1), peers)
+        pl.semaphore_signal(barrier, inc=1, device_id={"dom": to, "rep": r},
                             device_id_type=MESH)
 
     for other in (*r_way, r_pair):
@@ -93,7 +94,8 @@
         @pl.loop(0, peers)
         def _(n):
             pl.semaphore_signal(barrier, inc=1,
-                                device_id={"dom": wrap(d + n, peers), "rep": r_pair},
+                                device_id={"dom": wrap(d + n + peers // 2 - 4, peers),
+                                           "rep": r_pair},
                                 device_id_type=MESH)
 
     loads[0].wait()
@@ -110,6 +112,25 @@
         hot = jnp.where(rows == target, 1.0, 0.0).astype(bf16)
         ordered[pl.ds(pl.multiple_of(t * tile, tile), tile), :] = lax.dot_general(
             hot, grad_ref[...], (((1,), (0,)), ((), ())), preferred_element_type=f32).astype(bf16)
+
+    pl.semaphore_wait(barrier, peers - 1 + 3 + group)
+
+    own = pltpu.make_async_copy(
+        ordered.at[pl.ds(pl.multiple_of(d * piece, piece), piece)], raw.at[z, x, r], own_sem)
+    own.start()
+
+    def a_copy(n, zs, xs):
+        j, i = n // xs_n, lax.rem(n, xs_n)
+        to = wrap(z + offset(j), zs_n) * xs_n + wrap(x + i, xs_n)
+        return pltpu.make_async_remote_copy(
+            src_ref=ordered.at[pl.ds(pl.multiple_of(to * piece, piece), piece)],
+            dst_ref=raw.at[zs, xs, r],
+            send_sem=a_send.at[n], recv_sem=a_recv.at[n],
+            device_id={"dom": to, "rep": r}, device_id_type=MESH)
+
+    @pl.loop(1, peers)
+    def _(n):
+        a_copy(n, z, x).start()
 
     loads[2].wait()
     table_ref[...] = make_table(index_ref[...], count_ref[0])
@@ -119,25 +140,6 @@
     p = lax.broadcasted_iota(jnp.int32, (tile, tile), 1)
     wanted = lax.rem(q // slot_rows, 8) * piece + (q // piece) * slot_rows + lax.rem(q, slot_rows)
     unperm[...] = jnp.where(p == wanted, 1.0, 0.0).astype(bf16)
-
-    pl.semaphore_wait(barrier, peers - 1 + 3 + group)
-
-    own = pltpu.make_async_copy(
-        ordered.at[pl.ds(pl.multiple_of(d * piece, piece), piece)], raw.at[z, x, r], own_sem)
-    own.start()
-
-    def a_copy(n, zs, xs):
-        j, i = n // xs_n, lax.rem(n, xs_n)
-        to = wrap(z + offset(j), zs_n) * xs_n + wrap(x + i, xs_n)
-        return pltpu.make_async_remote_copy(
-            src_ref=ordered.at[pl.ds(pl.multiple_of(to * piece, piece), piece)],
-            dst_ref=raw.at[zs, xs, r],
-            send_sem=a_send.at[n], recv_sem=a_recv.at[n],
-            device_id={"dom": to, "rep": r}, device_id_type=MESH)
-
-    @pl.loop(1, peers)
-    def _(n):
-        a_copy(n, z, x).start()
 
     def chunk_of(j):
         return wrap(z - offset(j), zs_n)
@@ -435,10 +437,34 @@
     )(*args)
 
 
+def store_kernel(gi_ref, sum_ref, gi_hbm, sum_hbm, sems):
+    copies = [pltpu.make_async_copy(gi_ref, gi_hbm, sems.at[0]),
+              pltpu.make_async_copy(sum_ref, sum_hbm, sems.at[1])]
+    for copy in copies:
+        copy.start()
+    for copy in copies:
+        copy.wait()
+
+
+def store(*values):
+    vmem = pl.BlockSpec(memory_space=pltpu.VMEM)
+    far = pl.BlockSpec(memory_space=pltpu.HBM)
+    return pl.pallas_call(
+        store_kernel,
+        out_shape=tuple(jax.ShapeDtypeStruct(a.shape, a.dtype) for a in values),
+        in_specs=[vmem, vmem],
+        out_specs=(far, far),
+        scratch_shapes=[pltpu.SemaphoreType.DMA((2,))],
+        compiler_params=pltpu.CompilerParams(vmem_limit_bytes=4 << 20),
+        name="store",
+    )(*values)
+
+
 def on_device(grad_out, features, weight, edge_blocks, block_index, block_count, node_perm):
     nodes = grad_out.shape[0] * lax.axis_size("dom") * lax.axis_size("rep")
-    return layer(node_perm, grad_out, block_index.T, block_count, edge_blocks, features, weight,
-                 1.0 / math.sqrt(nodes))
+    return store(*layer(
+        node_perm, grad_out, block_index.T, block_count, edge_blocks, features, weight,
+        1.0 / math.sqrt(nodes)))
 
 
 def solution(mesh):

time: 85.1 us -> 83.9 us (0.986)
  local copies, waits for them, and re-layouts: 1.57 us -> 0 us
    unnamed x2 -> x0, local copies, waits for them, and re-layouts: 1.57 us -> none
    pallas_call x0 -> x1, Pallas kernels: none -> 0.99 us  [store(): pl.pallas_call(store_kernel, out_shape=tuple((jax.ShapeDtypeStruct(a.shap...]
where the time goes in v8:
time: 83.9 us; the launch traced here: 83.8 us
  Pallas kernels  82.5 us (98%)
  between operations  1.29 us (2%)
    pallas_call x1, Pallas kernels, layer(): pl.pallas_call(lambda *refs: layer_kernel(zs_n, xs_n, ys_n, scale, *refs)...  81.6 us

profile of v8, /device:TPU:1, one launch (start us, length us, event | category | flops | bytes accessed | tf_op | source)
XLA Modules:
  0.0 83.8 jit_solution(16167478098456028344)
XLA Ops:
  1.3 81.6 %layer.1 = (bf16[1024,512]{1,0:T(8,128)(2,1)S(1)}, f32[16,64]{1,0:T(8,128)S(1)}) custom-call(s32[1,1024]{1,0:T(1,128)} %bitcast.2, bf16[1024,512]{1,0:T(8,128)(2,1)} %refs_1_.1, s32[2,128]{1,0:T(2,128)} %bitcast.3, s32[1]{0:T(128)S(6)} %copy.9.refs_3_, bf16[128,128,128]{2,1,0:T(8,128)(2,1)} %refs_4_.1, bf16[1024,512]{1,0:T(8,128)(2,1)} %refs_5_.1, ...), custom_call_target="tpu_custom_call" | custom-call | tf_op jit(solution)/shard_map/layer/pallas_call | solution.py:398
  82.8 1.0 %store.1 = (bf16[1024,512]{1,0:T(8,128)(2,1)}, f32[16,64]{1,0:T(8,128)}) custom-call(bf16[1024,512]{1,0:T(8,128)(2,1)S(1)} %get-tuple-element.4.gi_ref, f32[16,64]{1,0:T(8,128)S(1)} %get-tuple-element.5.sum_ref), custom_call_target="tpu_custom_call" | custom-call | tf_op jit(solution)/shard_map/store/pallas_call | solution.py:452

commit v9 on v8

--- a/solution.py
+++ b/solution.py
@@ -46,7 +46,7 @@
         zs_n, xs_n, ys_n, scale,
         perm_hbm, grad_hbm, index_hbm, count_ref, edge_hbm, feat_hbm,
         weight_hbm, gi_ref, out_ref,
-        perm_ref, grad_ref, index_ref, edge_ref, feat_ref, weight_ref, ordered, raw, unperm,
+        perm_ref, grad_ref, index_ref, edge_ref, feat_ref, weight_ref, feat_cols, ordered, raw, unperm,
         table_ref, tab, running, summed, dense, chunk, acc, agg_ref,
         part_other, part_mine, pair_in, sums, far_in, y_in, cols_sum, packed, dom_in,
         load_sem, own_sem, tab_sem, a_send, a_recv, y_send, y_recv, f_send, f_recv, p_send, p_recv,
@@ -215,6 +215,11 @@
         @pl.when(step < 3)
         def _():
             sum_pairs(step + 1)
+
+        @pl.when(step == 1)
+        def _():
+            loads[4].wait()
+            feat_cols[...] = feat_ref[...].T
 
         @pl.when(step >= 3)
         def _():
@@ -250,16 +255,15 @@
             p_copy(j, 3, r_far).start()
 
     agg_ref[...] = acc[...].astype(bf16)
-    for load in loads[4:]:
-        load.wait()
+    loads[5].wait()
     out_rows = out_ref.shape[0]
     tall, lanes = cols_sum.shape
     mid = tall // 2
 
     def partial(half):
-        cols = feat_ref[:, pl.ds(pl.multiple_of(half * tall, tall), tall)]
+        cols = feat_cols[pl.ds(pl.multiple_of(half * tall, tall), tall), :]
         return lax.dot_general(
-            cols, agg_ref[...], (((0,), (0,)), ((), ())),
+            cols, agg_ref[...], (((1,), (0,)), ((), ())),
             preferred_element_type=jnp.float32) * scale
 
     part_other[...] = partial(1 - c)
@@ -332,26 +336,6 @@
     gi_ref[...] = lax.dot_general(
         agg_ref[...], weight_ref[...], (((1,), (1,)), ((), ())),
         preferred_element_type=f32).astype(gi_ref.dtype)
-
-    @pl.when(c == home)
-    def _():
-        dom_in[d] = packed[c, d - c * group]
-
-    @pl.loop(0, peers)
-    def _(s):
-        @pl.when((s != d) | (c != home))
-        def _():
-            pltpu.make_async_remote_copy(
-                src_ref=packed.at[0, 0], dst_ref=dom_in.at[s],
-                send_sem=d_send.at[0, 0], recv_sem=d_recv.at[s],
-                device_id={"dom": d, "rep": r_pair}, device_id_type=MESH).wait_recv()
-
-    sums_of = [dom_in[s] for s in range(peers)]
-    while len(sums_of) > 1:
-        sums_of = [a + b for a, b in zip(sums_of[::2], sums_of[1::2])]
-    total = sums_of[0]
-    out_ref[:out_rows // 2] = total[:, :lanes // 2]
-    out_ref[out_rows // 2:] = total[:, lanes // 2:]
 
     for n in range(ys_n):
         c_copy(n).wait_send()
@@ -377,6 +361,26 @@
             f_copy(j, way, r).wait_send()
         for which in range(4):
             p_copy(j, which, r).wait_send()
+
+    @pl.when(c == home)
+    def _():
+        dom_in[d] = packed[c, d - c * group]
+
+    @pl.loop(0, peers)
+    def _(s):
+        @pl.when((s != d) | (c != home))
+        def _():
+            pltpu.make_async_remote_copy(
+                src_ref=packed.at[0, 0], dst_ref=dom_in.at[s],
+                send_sem=d_send.at[0, 0], recv_sem=d_recv.at[s],
+                device_id={"dom": d, "rep": r_pair}, device_id_type=MESH).wait_recv()
+
+    sums_of = [dom_in[s] for s in range(peers)]
+    while len(sums_of) > 1:
+        sums_of = [a + b for a, b in zip(sums_of[::2], sums_of[1::2])]
+    total = sums_of[0]
+    out_ref[:out_rows // 2] = total[:, :lanes // 2]
+    out_ref[out_rows // 2:] = total[:, lanes // 2:]
 
 
 def layer(perm, grad, index, count, edge, feat, weight, scale):
@@ -408,6 +412,7 @@
             pltpu.VMEM(edge.shape, bf16),
             pltpu.VMEM(feat.shape, bf16),
             pltpu.VMEM(weight.shape, bf16),
+            pltpu.VMEM(feat.shape[::-1], bf16),
             pltpu.VMEM((rows, width), bf16),
             pltpu.VMEM((zs_n, xs_n, reps, piece, width), bf16),
             pltpu.VMEM((256, 256), bf16),

time: 83.9 us -> 83.4 us (level)
  no operation moved by 1% of the time
where the time goes in v9:
time: 83.4 us; the launch traced here: 83.3 us
  Pallas kernels  82 us (98%)
  between operations  1.29 us (2%)
    pallas_call x1, Pallas kernels, layer(): pl.pallas_call(lambda *refs: layer_kernel(zs_n, xs_n, ys_n, scale, *refs)...  81 us

profile of v9, /device:TPU:1, one launch (start us, length us, event | category | flops | bytes accessed | tf_op | source)
XLA Modules:
  0.0 83.3 jit_solution(17792605437541299627)
XLA Ops:
  1.3 81.0 %layer.1 = (bf16[1024,512]{1,0:T(8,128)(2,1)S(1)}, f32[16,64]{1,0:T(8,128)S(1)}) custom-call(s32[1,1024]{1,0:T(1,128)} %bitcast.2, bf16[1024,512]{1,0:T(8,128)(2,1)} %refs_1_.1, s32[2,128]{1,0:T(2,128)} %bitcast.3, s32[1]{0:T(128)S(6)} %copy.9.refs_3_, bf16[128,128,128]{2,1,0:T(8,128)(2,1)} %refs_4_.1, bf16[1024,512]{1,0:T(8,128)(2,1)} %refs_5_.1, ...), custom_call_target="tpu_custom_call" | custom-call | tf_op jit(solution)/shard_map/layer/pallas_call | solution.py:402
  82.3 1.0 %store.1 = (bf16[1024,512]{1,0:T(8,128)(2,1)}, f32[16,64]{1,0:T(8,128)}) custom-call(bf16[1024,512]{1,0:T(8,128)(2,1)S(1)} %get-tuple-element.4.gi_ref, f32[16,64]{1,0:T(8,128)S(1)} %get-tuple-element.5.sum_ref), custom_call_target="tpu_custom_call" | custom-call | tf_op jit(solution)/shard_map/store/pallas_call | solution.py:457
